TPU v7x, 32 devices: a whole 2x2x4 slice. The times are simulated.
32 devices in a mesh: seq: 8 (over z, y), kv: 4 (over x, core).
Axes of the slice: x: 2, y: 2, z: 4, core: 2. Of those that a mesh axis runs over, the one named last changes fastest.
Arguments:
- tokens: bfloat16 [8192, 2048], P(('seq', 'kv')), may hold values from -6 to 6
- cotangent: bfloat16 [8192, 2048], P(('seq', 'kv')), may hold values from -6 to 6
- corpus_id: int32 [8], P('seq'), may hold values from 0 to 7
- corpus_weight: float32 [8], replicated, may hold values from 0.5 to 2
- step_count: int32 [1], replicated, may hold values from 1 to 20
- qkv_weight: float32 [2048, 1920], P(('seq', 'kv')), may hold values from -0.125 to 0.125
- out_weight: float32 [1280, 2048], P(('seq', 'kv')), may hold values from -1.25 to 1.25
- gains: float32 [4224], P(('seq', 'kv')), may hold values from 0.5 to 1.5
- gate_weight: float32 [2048, 5632], P('seq', 'kv'), may hold values from -0.125 to 0.125
- up_weight: float32 [2048, 5632], P('seq', 'kv'), may hold values from -0.125 to 0.125
- down_weight: float32 [2048, 5632], P('seq', 'kv'), may hold values from -0.078125 to 0.078125
- first_qkv: float32 [2048, 1920], P(('seq', 'kv')), may hold values from -64 to 64
- first_out: float32 [1280, 2048], P(('seq', 'kv')), may hold values from -8 to 8
- first_gains: float32 [4224], P(('seq', 'kv')), may hold values from -96 to 96
- first_gate: float32 [2048, 5632], P('seq', 'kv'), may hold values from -16 to 16
- first_up: float32 [2048, 5632], P('seq', 'kv'), may hold values from -16 to 16
- first_down: float32 [2048, 5632], P('seq', 'kv'), may hold values from -40 to 40
- second_qkv: float32 [2048, 1920], P(('seq', 'kv')), may hold values from 434.176 to 1720.32
- second_out: float32 [1280, 2048], P(('seq', 'kv')), may hold values from 9.8304 to 38.5024
- second_gains: float32 [4224], P(('seq', 'kv')), may hold values from 983.04 to 3850.24
- second_gate: float32 [2048, 5632], P('seq', 'kv'), may hold values from 39.3216 to 155.648
- second_up: float32 [2048, 5632], P('seq', 'kv'), may hold values from 39.3216 to 155.648
- second_down: float32 [2048, 5632], P('seq', 'kv'), may hold values from 212.992 to 819.2
Outputs:
- block_out: bfloat16 [8192, 2048], P(('seq', 'kv'))
- grad_input: float32 [8192, 2048], P(('seq', 'kv'))
- new_qkv: float32 [2048, 1920], P(('seq', 'kv'))
- moments_qkv: float32 [2, 2048, 1920], P(None, ('seq', 'kv'))
- new_out: float32 [1280, 2048], P(('seq', 'kv'))
- moments_out: float32 [2, 1280, 2048], P(None, ('seq', 'kv'))
- new_gains: float32 [4224], P(('seq', 'kv'))
- moments_gains: float32 [2, 4224], P(None, ('seq', 'kv'))
- new_gate: float32 [2048, 5632], P('seq', 'kv')
- moments_gate: float32 [2, 2048, 5632], P(None, 'seq', 'kv')
- new_up: float32 [2048, 5632], P('seq', 'kv')
- moments_up: float32 [2, 2048, 5632], P(None, 'seq', 'kv')
- new_down: float32 [2048, 5632], P('seq', 'kv')
- moments_down: float32 [2, 2048, 5632], P(None, 'seq', 'kv')
All inputs are finite; a program needn't handle non-finite values.
Results may differ from a plain program's by a relative error of at most 0.014.
The roundings to bfloat16 on the way count: a program that leaves them out, or rounds other values in their place, can miss the bound.
Values may be sent and summed in bfloat16 or wider, within the bound.
No kernel may reach another device: no remote copies, remote signals or barrier semaphores. Data moves between devices by JAX's collectives and lax.ppermute only.
A program may use at most 256 MiB of HBM per device.

v0:
```python
import functools

import jax
import jax.numpy as jnp
import numpy as np
from jax import lax
from jax.experimental import pallas as pl
from jax.experimental.pallas import tpu as pltpu
from jax.sharding import Mesh, PartitionSpec as P

QUERY_HEADS = 20
VALUE_GROUPS = 5
HEAD_SIZE = 64

eps_norm = 1e-06
masked_value = -1e30
beta_first = 0.9
beta_second = 0.95
adam_eps = 1e-08

ALL = ("sh", "sl", "kh", "kl")
SEQ = ("sh", "sl")
KV = ("kh", "kl")
OWNERS = ("sh", "kl")
VMEM_LIMIT = 40 * 1024 * 1024
GAIN_ROWS = 8


def rms_scale(value_rows):
    return lax.rsqrt(jnp.mean(value_rows * value_rows, -1, keepdims=True) + eps_norm)


def norm_back(grad_out, value_rows, scale, gain):
    shaped = value_rows * scale
    pushed = grad_out * gain
    grad_in = scale * (pushed - shaped * jnp.mean(pushed * shaped, -1, keepdims=True))
    return (grad_in, grad_out * shaped)


def angle_tables(item_count):
    places = np.arange(item_count).astype(np.float32)
    steps = np.arange(HEAD_SIZE // 2).astype(np.float32) * np.float32(2.0) / np.float32(HEAD_SIZE)
    freqs = np.float32(10000.0) ** (-steps)
    angles = freqs[:, None].astype(np.float32) * places[None, :]
    return (np.cos(angles).astype(np.float32), np.sin(angles).astype(np.float32))


def contract(left, right, left_dim, right_dim):
    return lax.dot_general(
        left,
        right,
        (((left_dim,), (right_dim,)), ((), ())),
        preferred_element_type=jnp.float32,
    )


def head_scale(rows):
    return lax.rsqrt(jnp.mean(rows * rows, 0, keepdims=True) + eps_norm)


def rotated(rows, scale, gain, cosine, sine):
    half = HEAD_SIZE // 2
    shaped = rows * scale * gain
    first, second = shaped[:half], shaped[half:]
    return jnp.concatenate(
        [first * cosine - second * sine, second * cosine + first * sine], axis=0
    )


def unrotated_norm_back(grad, rows, scale, gain, cosine, sine):
    half = HEAD_SIZE // 2
    first, second = grad[:half], grad[half:]
    turned = jnp.concatenate(
        [first * cosine + second * sine, second * cosine - first * sine], axis=0
    )
    shaped = rows * scale
    pushed = turned * gain
    grad_in = scale * (pushed - shaped * jnp.mean(pushed * shaped, 0, keepdims=True))
    return (grad_in, turned * shaped)


def causal(block):
    keys = lax.broadcasted_iota(jnp.int32, (block, block), 0)
    places = lax.broadcasted_iota(jnp.int32, (block, block), 1)
    return keys <= places


def forward_kernel(
    group_ref, qp_ref, kp_ref, vp_ref, cos_ref, sin_ref, gq_ref, gk_ref,
    q_ref, k_ref, v_ref, out_ref, lse_ref, *, block,
):
    cosine, sine = cos_ref[...], sin_ref[...]
    qp, kp = qp_ref[...], kp_ref[...]
    query = (rotated(qp, head_scale(qp), gq_ref[...], cosine, sine) * 0.125).astype(jnp.bfloat16)
    key = rotated(kp, head_scale(kp), gk_ref[...], cosine, sine).astype(jnp.bfloat16)
    value = vp_ref[...].astype(jnp.bfloat16)
    q_ref[0] = query
    k_ref[0] = key
    v_ref[0] = value
    allowed = causal(block)
    for index in range(query.shape[1] // block):
        start, stop = index * block, (index + 1) * block
        part = query[:, start:stop]
        near = contract(key[:, start:stop], part, 0, 0)
        near = jnp.where(allowed, near, masked_value)
        top = jnp.max(near, 0, keepdims=True)
        if index:
            far = contract(key[:, :start], part, 0, 0)
            top = jnp.maximum(top, jnp.max(far, 0, keepdims=True))
        near = jnp.exp(near - top)
        total = jnp.sum(near, 0, keepdims=True)
        if index:
            far = jnp.exp(far - top)
            total = total + jnp.sum(far, 0, keepdims=True)
        share = 1.0 / total
        result = contract(value[:, start:stop], (near * share).astype(jnp.bfloat16), 1, 0)
        if index:
            result = result + contract(value[:, :start], (far * share).astype(jnp.bfloat16), 1, 0)
        out_ref[index] = result.astype(jnp.bfloat16)
        lse_ref[0, :, start:stop] = top + jnp.log(total)


def backward_kernel(
    group_ref, qp_ref, kp_ref, q_ref, k_ref, v_ref, do_ref, lse_ref, cos_ref, sin_ref,
    gq_ref, gk_ref,
    gqp_ref, gkp_ref, gv_ref, gain_q_ref, gain_k_ref,
    dq_ref, dk_ref, dv_ref, sum_q_ref, sum_k_ref, *, block,
):
    head = pl.program_id(0)
    heads = pl.num_programs(0)
    group = group_ref[head]
    opens = jnp.logical_or(head == 0, group_ref[jnp.maximum(head - 1, 0)] != group)
    closes = jnp.logical_or(
        head == heads - 1, group_ref[jnp.minimum(head + 1, heads - 1)] != group
    )

    @pl.when(head == 0)
    def _():
        sum_q_ref[...] = jnp.zeros_like(sum_q_ref)
        sum_k_ref[...] = jnp.zeros_like(sum_k_ref)

    @pl.when(opens)
    def _():
        dk_ref[...] = jnp.zeros_like(dk_ref)
        dv_ref[...] = jnp.zeros_like(dv_ref)

    query, key, value = q_ref[0], k_ref[0], v_ref[0]
    allowed = causal(block)
    for index in range(query.shape[1] // block):
        start, stop = index * block, (index + 1) * block
        part, grad_part = query[:, start:stop], do_ref[index]
        sums_log = lse_ref[0, :, start:stop]
        near = jnp.exp(contract(key[:, start:stop], part, 0, 0) - sums_log)
        near = jnp.where(allowed, near, 0.0)
        grad_near = contract(value[:, start:stop], grad_part, 0, 0)
        inner = jnp.sum(near * grad_near, 0, keepdims=True)
        if index:
            far = jnp.exp(contract(key[:, :start], part, 0, 0) - sums_log)
            grad_far = contract(value[:, :start], grad_part, 0, 0)
            inner = inner + jnp.sum(far * grad_far, 0, keepdims=True)
        step = (near * (grad_near - inner)).astype(jnp.bfloat16)
        total = contract(key[:, start:stop], step, 1, 0)
        dk_ref[:, start:stop] += contract(part, step, 1, 1)
        dv_ref[:, start:stop] += contract(grad_part, near.astype(jnp.bfloat16), 1, 1)
        if index:
            step = (far * (grad_far - inner)).astype(jnp.bfloat16)
            total = total + contract(key[:, :start], step, 1, 0)
            dk_ref[:, :start] += contract(part, step, 1, 1)
            dv_ref[:, :start] += contract(grad_part, far.astype(jnp.bfloat16), 1, 1)
        dq_ref[:, start:stop] = total * 0.125

    cosine, sine = cos_ref[...], sin_ref[...]
    qp = qp_ref[...]
    grad_qp, gain_terms = unrotated_norm_back(
        dq_ref[...].astype(jnp.bfloat16).astype(jnp.float32),
        qp, head_scale(qp), gq_ref[...], cosine, sine,
    )
    gqp_ref[...] = grad_qp.astype(jnp.bfloat16)
    sum_q_ref[...] += gain_terms

    @pl.when(closes)
    def _():
        kp = kp_ref[...]
        grad_kp, terms = unrotated_norm_back(
            dk_ref[...].astype(jnp.bfloat16).astype(jnp.float32),
            kp, head_scale(kp), gk_ref[...], cosine, sine,
        )
        gkp_ref[0] = grad_kp.astype(jnp.bfloat16)
        gv_ref[0] = dv_ref[...].astype(jnp.bfloat16)
        sum_k_ref[...] += terms

    @pl.when(head == heads - 1)
    def _():
        gain_q_ref[...] = jnp.sum(sum_q_ref[...], 1, keepdims=True)
        gain_k_ref[...] = jnp.sum(sum_k_ref[...], 1, keepdims=True)


def attention_specs(length, heads, block):
    half = HEAD_SIZE // 2
    tall = (HEAD_SIZE, length)
    whole = lambda shape: pl.BlockSpec(shape, lambda h, g: (0, 0))
    per_head = pl.BlockSpec((1,) + tall, lambda h, g: (h, 0, 0))
    per_group = pl.BlockSpec((1,) + tall, lambda h, g: (g[h], 0, 0))
    per_row = pl.BlockSpec((1, 1, length), lambda h, g: (h, 0, 0))
    query = pl.BlockSpec(tall, lambda h, g: (h, 0))
    key = pl.BlockSpec(tall, lambda h, g: (heads + g[h], 0))
    value = pl.BlockSpec(tall, lambda h, g: (heads + 2 + g[h], 0))
    table = whole((half, length))
    gain = whole((HEAD_SIZE, 1))
    per_owner = pl.BlockSpec((length // block, HEAD_SIZE, block), lambda h, g: (0, h, 0))
    return (query, key, value, per_head, per_group, per_row, table, gain, per_owner)


def attend(groups, mixed, cosine, sine, gain_q, gain_k, heads, block):
    length = mixed.shape[1]
    query, key, value, per_head, per_group, per_row, table, gain, per_owner = attention_specs(
        length, heads, block
    )
    per = lambda count: jax.ShapeDtypeStruct((count, HEAD_SIZE, length), jnp.bfloat16)
    scores = heads * length * length // 2
    return pl.pallas_call(
        functools.partial(forward_kernel, block=block),
        name="attention_forward",
        out_shape=(
            per(heads), per(2), per(2),
            jax.ShapeDtypeStruct((length // block, heads * HEAD_SIZE, block), jnp.bfloat16),
            jax.ShapeDtypeStruct((heads, 1, length), jnp.float32),
        ),
        grid_spec=pltpu.PrefetchScalarGridSpec(
            num_scalar_prefetch=1,
            grid=(heads,),
            in_specs=[query, key, value, table, table, gain, gain],
            out_specs=[per_head, per_group, per_group, per_owner, per_row],
        ),
        compiler_params=pltpu.CompilerParams(
            dimension_semantics=("arbitrary",), vmem_limit_bytes=VMEM_LIMIT
        ),
        cost_estimate=pl.CostEstimate(
            flops=scores * 4 * HEAD_SIZE, transcendentals=scores, bytes_accessed=8_000_000
        ),
    )(groups, mixed, mixed, mixed, cosine, sine, gain_q, gain_k)


def attend_back(
    groups, mixed, query_rows, key_rows, value_rows, grads, lse, cosine, sine, gain_q, gain_k, heads, block
):
    length = mixed.shape[1]
    query, key, value, per_head, per_group, per_row, table, gain, per_owner = attention_specs(
        length, heads, block
    )
    tall = (HEAD_SIZE, length)
    scores = heads * length * length // 2
    return pl.pallas_call(
        functools.partial(backward_kernel, block=block),
        name="attention_backward",
        out_shape=(
            jax.ShapeDtypeStruct((heads * HEAD_SIZE, length), jnp.bfloat16),
            jax.ShapeDtypeStruct((2,) + tall, jnp.bfloat16),
            jax.ShapeDtypeStruct((2,) + tall, jnp.bfloat16),
            jax.ShapeDtypeStruct((HEAD_SIZE, 1), jnp.float32),
            jax.ShapeDtypeStruct((HEAD_SIZE, 1), jnp.float32),
        ),
        grid_spec=pltpu.PrefetchScalarGridSpec(
            num_scalar_prefetch=1,
            grid=(heads,),
            in_specs=[
                query, key, per_head, per_group, per_group, per_owner, per_row, table, table, gain, gain,
            ],
            out_specs=[query, per_group, per_group, gain, gain],
            scratch_shapes=[pltpu.VMEM(tall, jnp.float32)] * 5,
        ),
        compiler_params=pltpu.CompilerParams(
            dimension_semantics=("arbitrary",), vmem_limit_bytes=VMEM_LIMIT
        ),
        cost_estimate=pl.CostEstimate(
            flops=scores * 10 * HEAD_SIZE, transcendentals=scores, bytes_accessed=10_000_000
        ),
    )(groups, mixed, mixed, query_rows, key_rows, value_rows, grads, lse, cosine, sine, gain_q, gain_k)


def row_order_kernel(mine_ref, in_ref, out_ref, *, offsets, back):
    for index, offset in enumerate(offsets):
        held = mine_ref[0] ^ offset
        if back:
            out_ref[held] = in_ref[index]
        else:
            out_ref[index] = in_ref[held]


def column_order_kernel(mine_ref, in_ref, out_ref, *, lines, parts, back):
    width = in_ref.shape[1] // (2 * lines)
    small = width // parts
    for plane in range(2):
        for line in range(lines):
            held = pl.multiple_of((mine_ref[0] ^ (line * 2 + plane)) * width, width)
            places = [(plane * parts + part) * lines + line for part in range(parts)]
            if back:
                out_ref[:, pl.ds(held, width)] = jnp.concatenate(
                    [in_ref[:, at * small : (at + 1) * small] for at in places], axis=1
                )
            else:
                block = in_ref[:, pl.ds(held, width)]
                for part, at in enumerate(places):
                    out_ref[:, at * small : (at + 1) * small] = block[
                        :, part * small : (part + 1) * small
                    ]


def order_call(kernel, array, mine):
    return pl.pallas_call(
        kernel,
        name="block_order",
        out_shape=jax.ShapeDtypeStruct(array.shape, array.dtype),
        in_specs=[
            pl.BlockSpec(memory_space=pltpu.SMEM),
            pl.BlockSpec(memory_space=pltpu.VMEM),
        ],
        out_specs=pl.BlockSpec(memory_space=pltpu.VMEM),
        compiler_params=pltpu.CompilerParams(vmem_limit_bytes=VMEM_LIMIT),
        cost_estimate=pl.CostEstimate(
            flops=0, transcendentals=0, bytes_accessed=4 * array.size
        ),
    )(mine.reshape(1).astype(jnp.int32), array)


def column_order(array, mine, lines, parts, back=False):
    rows, columns = array.shape
    width = columns // (2 * lines)
    if width % 128 == 0:
        kernel = functools.partial(column_order_kernel, lines=lines, parts=parts, back=back)
        return order_call(kernel, array, mine)
    small = width // parts
    if back:
        array = array.reshape(rows, 2, parts, lines, small).transpose(0, 3, 1, 2, 4)
        return jnp.where(mine == 0, array, array[:, :, ::-1]).reshape(rows, columns)
    array = array.reshape(rows, lines, 2, parts, small)
    array = jnp.where(mine == 0, array, array[:, :, ::-1])
    return array.transpose(0, 2, 3, 1, 4).reshape(rows, columns)


def head_columns(part, width):
    keys_at = QUERY_HEADS * HEAD_SIZE + part * HEAD_SIZE
    values_at = keys_at + VALUE_GROUPS * HEAD_SIZE
    pair = 2 * HEAD_SIZE
    return ((part * width, 0, width), (keys_at, width, pair), (values_at, width + pair, pair))


def split_kernel(in_ref, qkv_ref, out_ref, gain_ref, *, width):
    parts, lines, rows, _ = qkv_ref.shape
    for line in range(lines):
        for part in range(parts):
            for source, target, count in head_columns(part, width):
                qkv_ref[part, line, :, target : target + count] = in_ref[
                    line, :rows, source : source + count
                ]
        out_ref[line] = in_ref[line, rows:, :]
        gain_ref[line] = in_ref[line, : gain_ref.shape[1], in_ref.shape[2] - gain_ref.shape[2] :]


def split_columns(both, parts, rows, width, gain_width):
    lines, total, model = both.shape
    span = width + 4 * HEAD_SIZE
    return pl.pallas_call(
        functools.partial(split_kernel, width=width),
        name="split_columns",
        out_shape=(
            jax.ShapeDtypeStruct((parts, lines, rows, span), both.dtype),
            jax.ShapeDtypeStruct((lines, total - rows, model), both.dtype),
            jax.ShapeDtypeStruct((lines, min(GAIN_ROWS, rows), gain_width), both.dtype),
        ),
        compiler_params=pltpu.CompilerParams(vmem_limit_bytes=VMEM_LIMIT),
        cost_estimate=pl.CostEstimate(
            flops=0, transcendentals=0, bytes_accessed=4 * both.size
        ),
    )(both)


def join_kernel(in_ref, qkv_ref, *, width):
    parts, lines, _, _ = in_ref.shape
    for line in range(lines):
        for part in range(parts):
            qkv_ref[line, :, part * width : (part + 1) * width] = in_ref[part, line, :, :width]
        for kind in range(2):
            for group in range(VALUE_GROUPS):
                terms = []
                for part in range(max(group - 1, 0), min(group + 1, parts)):
                    at = width + (2 * kind + group - part) * HEAD_SIZE
                    terms.append(in_ref[part, line, :, at : at + HEAD_SIZE].astype(jnp.float32))
                at = (QUERY_HEADS + kind * VALUE_GROUPS + group) * HEAD_SIZE
                qkv_ref[line, :, at : at + HEAD_SIZE] = sum(terms).astype(qkv_ref.dtype)


def join_columns(qkv_parts, width):
    _, lines, rows, _ = qkv_parts.shape
    shape = (lines, rows, (QUERY_HEADS + 2 * VALUE_GROUPS) * HEAD_SIZE)
    return pl.pallas_call(
        functools.partial(join_kernel, width=width),
        name="join_columns",
        out_shape=jax.ShapeDtypeStruct(shape, jnp.bfloat16),
        compiler_params=pltpu.CompilerParams(vmem_limit_bytes=VMEM_LIMIT),
        cost_estimate=pl.CostEstimate(
            flops=0, transcendentals=0, bytes_accessed=4 * int(np.prod(shape))
        ),
    )(qkv_parts)


def adamw_kernel(
    stays_ref, fixes_ref, weight_ref, own_ref, moved_ref, first_ref, second_ref, new_ref, moments_ref,
    *, rate, shrink,
):
    high = jnp.float32
    grad = jnp.where(stays_ref[0] == 1, own_ref[...].astype(high), moved_ref[...].astype(high))
    first_new = beta_first * first_ref[...] + (1.0 - beta_first) * grad
    second_new = beta_second * second_ref[...] + (1.0 - beta_second) * grad * grad
    stepped = first_new / fixes_ref[0] / (jnp.sqrt(second_new / fixes_ref[1]) + adam_eps)
    weight = weight_ref[...]
    new_ref[...] = weight - rate * (stepped + shrink * weight)
    moments_ref[0] = first_new
    moments_ref[1] = jnp.sqrt(second_new)


def adamw_block(weight, grads, first, second, rate, shrink, stays, fixes):
    rows, columns = weight.shape
    tile = 64 if rows % 64 == 0 else rows
    block = pl.BlockSpec((tile, columns), lambda i: (i, 0))
    scalar = pl.BlockSpec(memory_space=pltpu.SMEM)
    return pl.pallas_call(
        functools.partial(adamw_kernel, rate=rate, shrink=shrink),
        name="adamw",
        out_shape=(
            jax.ShapeDtypeStruct(weight.shape, weight.dtype),
            jax.ShapeDtypeStruct((2,) + weight.shape, weight.dtype),
        ),
        grid=(rows // tile,),
        in_specs=[scalar, scalar] + [block] * 5,
        out_specs=(block, pl.BlockSpec((2, tile, columns), lambda i: (0, i, 0))),
        compiler_params=pltpu.CompilerParams(vmem_limit_bytes=VMEM_LIMIT),
        cost_estimate=pl.CostEstimate(
            flops=20 * weight.size, transcendentals=2 * weight.size, bytes_accessed=28 * weight.size
        ),
    )(stays.reshape(1), fixes, weight, grads[0], grads[1], first, second)


def adamw(weight, grad, first, second, rate, shrink, item_count):
    first_new = beta_first * first + (1.0 - beta_first) * grad
    second_new = beta_second * second + (1.0 - beta_second) * grad * grad
    fix_first = 1.0 - jnp.power(beta_first, item_count)
    fix_second = 1.0 - jnp.power(beta_second, item_count)
    stepped = first_new / fix_first / (jnp.sqrt(second_new / fix_second) + adam_eps)
    return (
        weight - rate * (stepped + shrink * weight),
        jnp.stack([first_new, jnp.sqrt(second_new)]),
    )


def local(
    sizes,
    tokens,
    cotangent,
    corpus_id,
    corpus_weight,
    step_count,
    qkv_weight,
    out_weight,
    gains,
    gate_weight,
    up_weight,
    down_weight,
    first_qkv,
    first_out,
    first_gains,
    first_gate,
    first_up,
    first_down,
    second_qkv,
    second_out,
    second_gains,
    second_gate,
    second_up,
    second_down,
):
    low = jnp.bfloat16
    high = jnp.float32
    devices = int(np.prod(sizes))
    seqs = sizes[0] * sizes[1]
    parts = sizes[2] * sizes[3]
    places = np.arange(devices).reshape(sizes)
    where = np.stack(np.unravel_index(np.arange(devices), sizes), -1)

    def permute(array, target):
        pairs = [(int(i), int(places[tuple(target(*where[i]))])) for i in range(devices)]
        return lax.ppermute(array, ALL, [pair for pair in pairs if pair[0] != pair[1]])

    def swap(array):
        moved = permute(array, lambda sh, sl, kh, kl: (sh, kl, kh, sl))
        return jnp.where(lax.axis_index("sl") == lax.axis_index("kl"), array, moved)

    def in_ffn_group(array, r):
        return permute(array, lambda sh, sl, kh, kl: (sh, sl ^ (r & 1), kh ^ (r >> 1), kl))

    def in_sequence(array, r):
        return permute(array, lambda sh, sl, kh, kl: (sh, sl, kh ^ (r >> 1), kl ^ (r & 1)))

    def along_y(array):
        return permute(array, lambda sh, sl, kh, kl: (sh, sl ^ 1, kh, kl))

    z_size = sizes[0]

    def halve(blocks, index, axis, move):
        kept = lax.dynamic_index_in_dim(blocks, index, axis, keepdims=False)
        sent = lax.dynamic_index_in_dim(blocks, index ^ 1, axis, keepdims=False)
        return (kept.astype(high) + move(sent).astype(high)).astype(low)

    item_count, model = tokens.shape
    heads = QUERY_HEADS // parts
    width = heads * HEAD_SIZE
    pair = 2 * HEAD_SIZE
    keys_at = QUERY_HEADS * HEAD_SIZE
    values_at = keys_at + VALUE_GROUPS * HEAD_SIZE
    kv = lax.axis_index(KV)
    length = item_count * parts
    cosine, sine = angle_tables(length)
    groups = ((jnp.arange(heads, dtype=jnp.int32) + kv) // 4).astype(jnp.int32)

    def stage(ready, waiting):
        return lax.optimization_barrier((ready, waiting))

    row_offsets = [
        (z * 2 + rs) * parts + r1 * 2 + r0
        for r0 in range(2) for r1 in range(2) for rs in range(2) for z in range(z_size)
    ]

    def columns_moved(array, back=False):
        return column_order(array, lax.axis_index("sl"), z_size, parts, back=back)

    def rows_moved(array, back=False):
        blocks = array.reshape(devices, -1, item_count)
        kernel = functools.partial(row_order_kernel, offsets=tuple(row_offsets), back=back)
        mine = lax.axis_index("sl") * parts + kv
        return order_call(kernel, blocks, mine).reshape(-1, item_count)

    span = width + 2 * pair
    own_rows, total_columns = qkv_weight.shape
    spare = model - total_columns
    gain_rows = -(-gains.shape[0] // spare)
    gains_block = jnp.pad(gains.astype(low), (0, own_rows * spare - gains.shape[0]))
    both = jnp.concatenate(
        [
            jnp.concatenate([qkv_weight.astype(low), gains_block.reshape(own_rows, spare)], axis=1),
            out_weight.astype(low),
        ]
    )
    both_line = lax.all_to_all(
        jnp.broadcast_to(both[None], (z_size,) + both.shape), "sh", split_axis=0, concat_axis=0, tiled=True
    )
    tokens_near = columns_moved(tokens)
    tokens_far = in_sequence(tokens_near, 2)
    gate_block = swap(gate_weight.astype(low))
    factor = jnp.sum(
        jnp.where(jnp.arange(corpus_weight.shape[0]) == corpus_id[0], corpus_weight, 0.0)
    )
    weighted = cotangent.astype(high) * factor
    weighted_low = weighted.astype(low)
    weighted_one = in_ffn_group(weighted_low, 1)
    (both_line, tokens_far, gate_block, weighted_one), (up_low, tokens_near, weighted_low) = stage(
        (both_line, tokens_far, gate_block, weighted_one),
        (up_weight.astype(low), tokens_near, weighted_low),
    )
    gate_full = lax.all_gather(gate_block, OWNERS, axis=0, tiled=True)

    qkv_parts, out_line, gain_line = split_columns(both_line, parts, own_rows, width, spare)
    gain_line = gain_line[:, :gain_rows].reshape(z_size, -1)
    gain_pairs = jnp.stack([gain_line, in_sequence(gain_line, 1)])
    gain_pairs = jnp.stack([gain_pairs, in_sequence(gain_pairs, 2)])
    qkv_rows = lax.all_to_all(
        qkv_parts, KV, split_axis=0, concat_axis=0, tiled=True
    )
    tokens_pair = (in_sequence(tokens_near, 1), in_sequence(tokens_far, 1))
    up_block = swap(up_low)
    out_near = jnp.stack([out_line, along_y(out_line)])
    (qkv_rows, tokens_pair, gain_pairs, up_block, out_near), (down_low, own_cotangent) = stage(
        (qkv_rows, tokens_pair, gain_pairs, up_block, out_near), (down_weight.astype(low), cotangent)
    )
    up_full = lax.all_gather(up_block, OWNERS, axis=0, tiled=True)

    qkv_far = along_y(qkv_rows)
    cotangent_far, out_near = stage(in_ffn_group(own_cotangent, 2), out_near)
    weighted_far = (cotangent_far.astype(high) * factor).astype(low)
    out_far = in_sequence(out_near, 2)
    held = jnp.arange(2 * parts)
    mine = lax.axis_index("sl") * parts + kv
    selection = held[:, None] == (held[None, :] ^ mine)
    gain_blocks = jnp.stack([gain_pairs, along_y(gain_pairs)])[..., : gains.shape[0]]
    gain_values = contract(selection.astype(low), gain_blocks.reshape(2 * parts, -1), 1, 0)
    gain_values = gain_values.reshape(2, parts, z_size, -1).transpose(2, 0, 1, 3).reshape(-1)
    gain_one = gain_values[:model]
    gain_two = gain_values[model : 2 * model]
    gain_q = gain_values[2 * model : 2 * model + HEAD_SIZE].reshape(HEAD_SIZE, 1)
    gain_k = gain_values[2 * model + HEAD_SIZE :].reshape(HEAD_SIZE, 1)
    gain_moved = columns_moved(jnp.broadcast_to(gain_one[None], (8, model)))[:1]
    all_rows = jnp.zeros((parts, item_count, model), low)
    for r, piece in enumerate((tokens_near, tokens_pair[0], tokens_far, tokens_pair[1])):
        all_rows = lax.dynamic_update_slice_in_dim(all_rows, piece[None], kv ^ r, 0)
    all_rows = all_rows.reshape(length, model).astype(high)
    normed = (all_rows * rms_scale(all_rows) * gain_moved).astype(low)
    normed, qkv_rows = stage(normed, qkv_rows)
    qkv_full = jnp.concatenate([qkv_rows, qkv_far]).reshape(model, span)

    mixed = contract(qkv_full, normed, 0, 1)
    query_rows, key_rows, value_rows, outgoing, lse = attend(
        groups, mixed, cosine, sine, gain_q, gain_k, heads, item_count
    )
    weighted_two = in_ffn_group(weighted_far, 1)
    (outgoing, weighted_two), (out_near, down_low) = stage((outgoing, weighted_two), (out_near, down_low))
    weighted_rows = (jnp.concatenate([weighted_low, weighted_one, weighted_far]), weighted_two)

    down_block = swap(down_low)
    attended = rows_moved(
        lax.all_to_all(outgoing, KV, split_axis=0, concat_axis=0, tiled=True)
    )
    out_full = (out_near, out_far, in_sequence(out_near, 1), in_sequence(out_far, 1))
    out_full = [piece.reshape(-1, model) for piece in out_full]
    (attended, out_full), down_block = stage((attended, out_full), down_block)
    attended = attended.reshape(4, -1, item_count)
    down_full = lax.all_gather(down_block, OWNERS, axis=0, tiled=True)
    inputs = tokens.astype(high)
    hidden = inputs + sum(contract(attended[i], out_full[i], 0, 0) for i in range(4))

    scale_two = rms_scale(hidden)
    normed_two = (hidden * scale_two * gain_two).astype(low)
    ffn_moved = [in_ffn_group(normed_two, r) for r in (3, 1, 2)]
    ffn_rows = (jnp.concatenate([normed_two, ffn_moved[1], ffn_moved[2]]), ffn_moved[0])

    def activation(rows, gate_full, up_full):
        gate = contract(rows, gate_full, 1, 0)
        up_part = contract(rows, up_full, 1, 0)
        sigma = jax.nn.sigmoid(gate)
        return (gate, up_part, sigma, (gate * sigma * up_part).astype(low))

    def activation_back(rows, down_full, gate, up_part, sigma):
        grad_acted = contract(rows, down_full, 1, 0)
        grad_gate = (grad_acted * up_part * sigma * (1.0 + gate * (1.0 - sigma))).astype(low)
        return (grad_gate, (grad_acted * (gate * sigma)).astype(low))

    def weight_gradient(left, right):
        return sum(contract(left[i], right[i], 0, 0) for i in range(2)).astype(low)

    def share(grad):
        return lax.psum_scatter(grad, OWNERS, scatter_dimension=0, tiled=True)

    near = activation(ffn_rows[0], gate_full, up_full)
    near, (gate_full, up_full) = stage(near, (gate_full, up_full))
    far = activation(ffn_rows[1], gate_full, up_full)
    acted = (near[3], far[3])
    grad_down_low = weight_gradient(weighted_rows, acted)
    down_full, grad_down_low = stage(down_full, grad_down_low)
    grad_down_share = share(grad_down_low)
    far_gate, far_up = activation_back(weighted_rows[1], down_full, *far[:3])
    sent_far = (contract(far_gate, gate_full, 1, 1) + contract(far_up, up_full, 1, 1)).astype(low)
    sent_far, weighted_near = stage(sent_far, weighted_rows[0])
    received_far = in_ffn_group(sent_far, 3)
    near_gate, near_up = activation_back(weighted_near, down_full, *near[:3])
    rows_partial = (contract(near_gate, gate_full, 1, 1) + contract(near_up, up_full, 1, 1)).astype(low)
    received = [
        in_ffn_group(rows_partial[r * item_count : (r + 1) * item_count], r) for r in (1, 2)
    ]
    grad_gate, grad_up = (near_gate, far_gate), (near_up, far_up)
    (received_far, rows_partial), (grad_gate, grad_up) = stage(
        (received_far, rows_partial), (grad_gate, grad_up)
    )
    grad_gate_share = share(weight_gradient(ffn_rows, grad_gate))
    grad_up_low = weight_gradient(ffn_rows, grad_up)
    ffn_partial = [contract(part, down_full, 1, 1).astype(low) for part in acted]
    (received, grad_down_share), (grad_up_low, ffn_partial) = stage(
        (received, grad_down_share), (grad_up_low, ffn_partial)
    )
    received = received + [received_far]
    grad_up_share = share(grad_up_low)
    grad_normed_two = rows_partial[:item_count].astype(high) + sum(
        piece.astype(high) for piece in received
    )

    pushed_two, gain_two_terms = norm_back(grad_normed_two, hidden, scale_two, gain_two)
    grad_hidden = weighted + pushed_two
    hidden_low = grad_hidden.astype(low)

    attended_gradient = jnp.concatenate(
        [contract(piece, hidden_low, 1, 1).astype(low) for piece in out_full]
    )
    attended_gradient = rows_moved(attended_gradient, back=True)
    incoming = lax.all_to_all(
        attended_gradient.reshape(parts, width, item_count), KV, split_axis=0, concat_axis=0, tiled=True
    )
    ffn_blocks = ffn_partial[0].reshape(3, item_count, model)
    ffn_moved = [in_ffn_group(ffn_blocks[1], 1), in_ffn_group(ffn_partial[1], 1)]
    sent_out = [
        contract(attended[2 + r], hidden_low, 1, 0).astype(low) for r in range(2)
    ]
    kept_out = [
        contract(attended[r], hidden_low, 1, 0) for r in range(2)
    ]
    out_line = [
        (kept_out[r] + in_sequence(sent_out[r], 1).astype(high)).astype(low) for r in range(2)
    ]
    incoming, out_line = lax.optimization_barrier((incoming, out_line))

    out_moved = in_sequence(out_line[1], 2)
    grad_queries, grad_keys, grad_values, gain_q_sum, gain_k_sum = attend_back(
        groups, mixed, query_rows, key_rows, value_rows, incoming, lse,
        cosine, sine, gain_q, gain_k, heads, item_count,
    )
    grad_mixed = jnp.concatenate(
        [grad_queries, grad_keys.reshape(pair, length), grad_values.reshape(pair, length)], axis=0
    )
    half_model = model // 2
    grad_mixed, (ffn_moved, grad_gate_share) = stage(grad_mixed, (ffn_moved, grad_gate_share))
    mixer_sent = contract(normed[:, half_model:], grad_mixed, 0, 1).astype(low)
    (mixer_sent, grad_mixed), (out_line, ffn_blocks) = stage(
        (mixer_sent, grad_mixed), (out_line[0], ffn_blocks)
    )

    mixer_moved = along_y(mixer_sent)
    mixer_line = contract(normed[:, :half_model], grad_mixed, 0, 1)
    grad_normed = contract(grad_mixed, qkv_full, 0, 1).astype(low)
    grad_normed = grad_normed.reshape(2, 2, item_count, model)
    core = lax.axis_index("kl")
    normed_moved = in_sequence(lax.dynamic_index_in_dim(grad_normed, core ^ 1, 1, keepdims=False), 1)
    ffn_line = [
        ffn_blocks[2 * r].astype(high) + ffn_moved[r].astype(high) for r in range(2)
    ]
    mixer_line = lax.optimization_barrier(mixer_line)
    mixer_parts = (mixer_line + mixer_moved.astype(high)).astype(low)
    mixer_parts, (out_line, shares) = stage(
        mixer_parts, (out_line, (grad_down_share, grad_gate_share))
    )
    swapped = [permute(piece, lambda sh, sl, kh, kl: (sh, kl, kh, sl)) for piece in shares]
    ffn_moved = in_ffn_group(ffn_line[1].astype(low), 2)
    swapped, ffn_moved = stage(swapped, ffn_moved)

    mixer_parts = lax.all_to_all(
        mixer_parts.reshape(parts, z_size, -1, span), KV, split_axis=0, concat_axis=0, tiled=True
    )
    out_line = (out_line.astype(high) + out_moved.astype(high)).astype(low).reshape(2, z_size, -1, model)
    out_moved = along_y(out_line[1])
    qkv_line = join_columns(mixer_parts, width)
    qkv_line, (grad_normed, normed_moved, out_line, grad_up_share) = stage(
        qkv_line, (grad_normed, normed_moved, out_line[0], grad_up_share)
    )

    qkv_line = lax.all_to_all(qkv_line, "sh", split_axis=0, concat_axis=0, tiled=True)
    grad_normed = lax.dynamic_index_in_dim(grad_normed, core, 1, keepdims=False).astype(high)
    grad_normed = (grad_normed + normed_moved.astype(high)).astype(low)
    grad_normed = halve(grad_normed, lax.axis_index("kh"), 0, lambda v: in_sequence(v, 2)).astype(high)
    steps_done = step_count[0].astype(high)
    fixes = jnp.stack(
        [1.0 - jnp.power(beta_first, steps_done), 1.0 - jnp.power(beta_second, steps_done)]
    )
    grad_normed, fixes = stage(grad_normed, fixes)
    line = lax.axis_index("sh")

    def sum_line(blocks):
        total = lax.dynamic_index_in_dim(blocks, line, 0, keepdims=False).astype(high)
        for r in range(1, z_size):
            sent = lax.dynamic_index_in_dim(blocks, line ^ r, 0, keepdims=False)
            total = total + permute(sent, lambda sh, sl, kh, kl: (sh ^ r, sl, kh, kl)).astype(high)
        return total

    out_grad = sum_line((out_line.astype(high) + out_moved.astype(high)).astype(low))
    block_out = (hidden + (ffn_line[0] + ffn_moved.astype(high))).astype(low)
    qkv_grad = jnp.sum(qkv_line.astype(high), 0)
    grad_down, grad_gate_w = zip(shares, swapped)
    grad_up_w = (grad_up_share, permute(grad_up_share, lambda sh, sl, kh, kl: (sh, kl, kh, sl)))
    moved_inputs = tokens_near.astype(high)
    pushed_one, gain_one_terms = norm_back(
        grad_normed, moved_inputs, rms_scale(moved_inputs), gain_moved
    )
    grad_input = grad_hidden + columns_moved(pushed_one, back=True)
    gain_one_sum = columns_moved(
        jnp.broadcast_to(jnp.sum(gain_one_terms, 0)[None], (8, model)), back=True
    )[0]
    grad_gains = jnp.concatenate(
        [
            gain_one_sum,
            jnp.sum(gain_two_terms, 0),
            gain_q_sum.reshape(-1),
            gain_k_sum.reshape(-1),
        ]
    )
    grad_gains = grad_gains.reshape(z_size, 2, parts, -1).transpose(1, 2, 0, 3)
    grad_gains = lax.dot_general(
        selection.astype(high), grad_gains.reshape(2 * parts, -1), (((1,), (0,)), ((), ())),
        precision=lax.Precision.HIGHEST, preferred_element_type=high,
    ).reshape(2, 2, 2, -1)
    grad_gains = grad_gains[0] + along_y(grad_gains[1])
    grad_gains = grad_gains[:, 0] + in_sequence(grad_gains[:, 1], 1)
    grad_gains = grad_gains[0] + in_sequence(grad_gains[1], 2)
    gains_grad = sum_line(grad_gains.reshape(z_size, -1))

    new_qkv, moments_qkv = adamw(qkv_weight, qkv_grad, first_qkv, second_qkv, 0.02, 0.1, steps_done)
    new_out, moments_out = adamw(out_weight, out_grad, first_out, second_out, 0.2, 0.1, steps_done)
    new_gains, moments_gains = adamw(
        gains, gains_grad, first_gains, second_gains, 0.6, 0.0, steps_done
    )
    stays = (lax.axis_index("sl") == lax.axis_index("kl")).astype(jnp.int32)
    new_gate, moments_gate = adamw_block(
        gate_weight, grad_gate_w, first_gate, second_gate, 0.02, 0.1, stays, fixes
    )
    new_up, moments_up = adamw_block(
        up_weight, grad_up_w, first_up, second_up, 0.02, 0.1, stays, fixes
    )
    new_down, moments_down = adamw_block(
        down_weight, grad_down, first_down, second_down, 0.013, 0.1, stays, fixes
    )
    return (
        block_out,
        grad_input,
        new_qkv,
        moments_qkv,
        new_out,
        moments_out,
        new_gains,
        moments_gains,
        new_gate,
        moments_gate,
        new_up,
        moments_up,
        new_down,
        moments_down,
    )


def solution(mesh):
    seqs, parts = mesh.shape["seq"], mesh.shape["kv"]
    sizes = (seqs // 2, 2, parts // 2, 2)
    fine = Mesh(mesh.devices.reshape(sizes), ALL)
    rows = P(ALL, None)
    block = P(SEQ, KV)
    return jax.shard_map(
        functools.partial(local, sizes),
        mesh=fine,
        in_specs=(
            rows, rows, P(SEQ), P(), P(),
            rows, rows, P(ALL), block, block, block,
            rows, rows, P(ALL), block, block, block,
            rows, rows, P(ALL), block, block, block,
        ),
        out_specs=(
            rows, rows,
            rows, P(None, ALL, None),
            rows, P(None, ALL, None),
            P(ALL), P(None, ALL),
            block, P(None, SEQ, KV),
            block, P(None, SEQ, KV),
            block, P(None, SEQ, KV),
        ),
        check_vma=False,
    )
```

profile of v0, /device:TPU:0, one launch (start us, length us, event | category | flops | bytes accessed | tf_op | source)
XLA Modules:
  0.0 548.7 jit_solution(6682760341380234965)
XLA Ops:
  11.4 6.4 %all-to-all-start = ((bf16[4,104,2048]{2,1,0:T(8,128)(2,1)}), bf16[4,104,2048]{2,1,0:T(8,128)(2,1)}, u32[]{:S(2)}, u32[]{:S(2)}) async-start(bf16[4,104,2048]{2,1,0:T(8,128)(2,1)} %broadcast_in_dim.21), calls=%async_computation | async-start | bytes 3407872 | tf_op jit(solution)/shard_map/all_to_all | solution.py:553
  31.9 14.0 %collective-permute-done = bf16[256,2048]{1,0:T(8,128)(2,1)} collective-permute-done((bf16[256,2048]{1,0:T(8,128)(2,1)S(1)}, bf16[256,2048]{1,0:T(8,128)(2,1)}, u32[]{:S(2)}, u32[]{:S(2)}) %collective-permute-start) | collective-permute-done | bytes 1048608 | tf_op jit(solution)/shard_map/ppermute | solution.py:492
  45.8 8.4 %collective-permute-done.2 = bf16[256,2048]{1,0:T(8,128)(2,1)} collective-permute-done((bf16[256,2048]{1,0:T(8,128)(2,1)}, bf16[256,2048]{1,0:T(8,128)(2,1)}, u32[]{:S(2)}, u32[]{:S(2)}) %collective-permute-start.2) | collective-permute-done | bytes 1048608 | tf_op jit(solution)/shard_map/ppermute | solution.py:492
  80.5 12.7 %all-to-all-done.1 = bf16[4,4,64,576]{3,2,1,0:T(8,128)(2,1)} async-done(((bf16[4,4,64,576]{3,2,1,0:T(8,128)(2,1)}), bf16[4,4,64,576]{3,2,1,0:T(8,128)(2,1)}, u32[]{:S(2)}, u32[]{:S(2)}) %all-to-all-start.1) | async-done | bytes 1179680 | tf_op jit(solution)/shard_map/all_to_all | solution.py:575
  115.8 17.9 %collective-permute-done.11 = bf16[256,2048]{1,0:T(8,128)(2,1)} collective-permute-done((bf16[256,2048]{1,0:T(8,128)(2,1)S(1)}, bf16[256,2048]{1,0:T(8,128)(2,1)}, u32[]{:S(2)}, u32[]{:S(2)}) %collective-permute-start.11) | collective-permute-done | bytes 1048608 | tf_op jit(solution)/shard_map/ppermute | solution.py:492
  145.0 10.4 %attention_forward.1 = (bf16[5,64,1024]{2,1,0:T(8,128)(2,1)S(1)}, bf16[2,64,1024]{2,1,0:T(8,128)(2,1)S(1)}, bf16[2,64,1024]{2,1,0:T(8,128)(2,1)S(1)}, bf16[4,320,256]{2,1,0:T(8,128)(2,1)S(1)}, f32[5,1,1024]{2,1,0:T(1,128)S(1)}) custom-call(s32[5]{0:T(128)S(1)} %and_select_fusion.group_ref, f32[576,1024]{1,0:T(8,128)S(1)} %fusion.73.qp_ref.kp_ref.vp_ref, ...), custom_call_target="tpu_custom_call" | custom-call | flops 671088640 | bytes 8000000 | tf_op jit(solution)/shard_map/attention_forward/pallas_call | solution.py:221
  163.3 13.7 %all_to_all.30 = bf16[4,320,256]{2,1,0:T(8,128)(2,1)S(1)} all-to-all(bf16[4,320,256]{2,1,0:T(8,128)(2,1)S(1)} %get-tuple-element.128), channel_id=1, replica_groups=mesh['sh'=4,'sl'=2,'kh'=2,'kl'=2] {'kh','kl'}, dimensions={0} | all-to-all | bytes 1310720 | tf_op jit(solution)/shard_map/all_to_all | solution.py:619
  190.8 21.5 %collective-permute-done.17 = bf16[256,2048]{1,0:T(8,128)(2,1)S(1)} collective-permute-done((bf16[256,2048]{1,0:T(8,128)(2,1)S(1)}, bf16[256,2048]{1,0:T(8,128)(2,1)S(1)}, u32[]{:S(2)}, u32[]{:S(2)}) %collective-permute-start.17) | collective-permute-done | bytes 1048608 | tf_op jit(solution)/shard_map/ppermute | solution.py:492
  215.5 10.8 %fusion.64 = f32[768,1408]{1,0:T(8,128)} fusion(bf16[2048,1408]{1,0:T(8,128)(2,1)} %all-gather.6.cloned.1.call-done, bf16[256,2048]{1,0:T(8,128)(2,1)} %collective-permute-done.18, bf16[256,2048]{1,0:T(8,128)(2,1)S(1)} %collective-permute-done.17, bf16[256,2048]{1,0:T(8,128)(2,1)S(1)} %multiply_convert_fusion.3), kind=kOutput, calls=%fused_computation.171 | convolution fusion | flops 4438622208 | bytes 13238272 | tf_op jit(solution)/shard_map/dot_general | solution.py:49
  226.3 12.3 %multiply_convert_fusion.2 = (bf16[768,1408]{1,0:T(8,128)(2,1)S(1)}, f32[768,1408]{1,0:T(8,128)}, f32[768,1408]{1,0:T(8,128)}) fusion(f32[768,1408]{1,0:T(8,128)} %fusion.64, bf16[2048,1408]{1,0:T(8,128)(2,1)} %all-gather.8.cloned.1.call-done, bf16[256,2048]{1,0:T(8,128)(2,1)} %collective-permute-done.18, ...), kind=kOutput, calls=%fused_computation.10 | convolution fusion | flops 4445110272 | bytes 24051712 | tf_op jit(solution)/shard_map/dot_general | solution.py:49
  245.4 7.0 %fusion.62 = f32[2048,1408]{1,0:T(8,128)S(1)} fusion(bf16[768,1408]{1,0:T(8,128)(2,1)S(1)} %get-tuple-element.145, bf16[256,2048]{1,0:T(8,128)(2,1)} %multiply_convert_fusion.4, bf16[256,2048]{1,0:T(8,128)(2,1)} %collective-permute-done.2, bf16[256,2048]{1,0:T(8,128)(2,1)} %fusion.22), kind=kOutput, calls=%fused_computation.169 | convolution fusion | flops 4438622208 | bytes 16842752 | tf_op jit(solution)/shard_map/dot_general | solution.py:49
  252.3 5.5 add_convert_fusion.2
  260.5 6.9 %multiply_convert_fusion.5 = (bf16[256,1408]{1,0:T(8,128)(2,1)S(1)}, bf16[256,1408]{1,0:T(8,128)(2,1)S(1)}) fusion(f32[256,1408]{1,0:T(8,128)} %copy-done.96, f32[256,1408]{1,0:T(8,128)} %get-tuple-element.256, bf16[256,2048]{1,0:T(8,128)(2,1)} %collective-permute-done.12, bf16[2048,1408]{1,0:T(8,128)(2,1)} %all-gather.4.cloned.1.call-done), kind=kOutput, calls=%fused_computation.66 | convolution fusion | flops 1481080832 | bytes 11141120 | tf_op jit(solution)/shard_map/dot_general | solution.py:49
  272.2 8.4 %fusion.76 = f32[768,1408]{1,0:T(8,128)S(1)} fusion(bf16[768,2048]{1,0:T(8,128)(2,1)S(1)} %pad_maximum_fusion, bf16[2048,1408]{1,0:T(8,128)(2,1)} %all-gather.4.cloned.1.call-done), kind=kOutput, calls=%fused_computation.182 | convolution fusion | flops 4429185024 | bytes 13238272 | tf_op jit(solution)/shard_map/dot_general | solution.py:49
  287.2 8.5 %add_convert_fusion.3 = bf16[768,2048]{1,0:T(8,128)(2,1)S(1)} fusion(f32[768,2048]{1,0:T(8,128)S(1)} %fusion.77, bf16[768,1408]{1,0:T(8,128)(2,1)S(1)} %get-tuple-element.156, bf16[2048,1408]{1,0:T(8,128)(2,1)} %all-gather.8.cloned.1.call-done), kind=kOutput, calls=%fused_computation.7 | convolution fusion | flops 4432330752 | bytes 17367040 | tf_op jit(solution)/shard_map/dot_general | solution.py:49
  298.4 8.7 %add_convert_fusion = bf16[2048,1408]{1,0:T(8,128)(2,1)} fusion(f32[2048,1408]{1,0:T(8,128)S(1)} %fusion.79, bf16[768,1408]{1,0:T(8,128)(2,1)S(1)} %get-tuple-element.168, bf16[256,2048]{1,0:T(8,128)(2,1)} %collective-permute-done.18, bf16[256,2048]{1,0:T(8,128)(2,1)S(1)} %copy-done.93, bf16[256,2048]{1,0:T(8,128)(2,1)S(1)} %copy-done.77), kind=kOutput, calls=%fused_computation | convolution fusion | flops 4444389376 | bytes 22609920 | tf_op jit(solution)/shard_map/dot_general | solution.py:49
  311.4 5.4 convolution_convert_fusion.4
  316.9 6.8 %convolution_convert_fusion.1 = bf16[768,2048]{1,0:T(8,128)(2,1)} fusion(bf16[768,1408]{1,0:T(8,128)(2,1)S(1)} %copy-done.98, bf16[2048,1408]{1,0:T(8,128)(2,1)S(1)} %bitcast.231), kind=kOutput, calls=%fused_computation.15 | convolution fusion | flops 4430757888 | bytes 11075584 | tf_op jit(solution)/shard_map/dot_general | solution.py:49
  325.8 9.1 %add_convert_fusion.1 = bf16[2048,1408]{1,0:T(8,128)(2,1)} fusion(f32[2048,1408]{1,0:T(8,128)S(1)} %fusion.78, bf16[768,1408]{1,0:T(8,128)(2,1)S(1)} %copy-done.71, bf16[256,2048]{1,0:T(8,128)(2,1)} %collective-permute-done.18, bf16[256,2048]{1,0:T(8,128)(2,1)S(1)} %copy-done.94, bf16[256,2048]{1,0:T(8,128)(2,1)S(1)} %copy-done.78), kind=kOutput, calls=%fused_computation.1 | convolution fusion | flops 4444389376 | bytes 22609920 | tf_op jit(solution)/shard_map/dot_general | solution.py:49
  340.5 5.7 %fusion.66 = (bf16[256,2048]{1,0:T(8,128)(2,1)S(1)}, f32[256,2048]{1,0:T(8,128)}) fusion(f32[256]{0:T(256)S(1)} %broadcast_multiply_fusion.1, f32[256,2048]{1,0:T(8,128)S(1)} %copy-done.47, f32[2048]{0:T(1024)S(1)} %get-tuple-element.238, bf16[256,2048]{1,0:T(8,128)(2,1)} %collective-permute-done.20, bf16[256,2048]{1,0:T(8,128)(2,1)} %collective-permute-done.22, ...), kind=kLoop, calls=%fused_computation.172 | loop fusion | flops 8388608 | bytes 10496004 | tf_op jit(solution)/shard_map/convert_element_type | solution.py:685
  382.4 15.8 %attention_backward.1 = (bf16[320,1024]{1,0:T(8,128)(2,1)S(1)}, bf16[2,64,1024]{2,1,0:T(8,128)(2,1)S(1)}, bf16[2,64,1024]{2,1,0:T(8,128)(2,1)S(1)}, f32[64,1]{1,0:T(8,128)S(1)}, f32[64,1]{1,0:T(8,128)S(1)}) custom-call(s32[5]{0:T(128)S(1)} %copy-done.44, f32[576,1024]{1,0:T(8,128)S(1)} %copy-done.1, f32[576,1024]{1,0:T(8,128)S(1)} %copy-done.1, ...), custom_call_target="tpu_custom_call" | custom-call | flops 1677721600 | bytes 10000000 | tf_op jit(solution)/shard_map/attention_backward/pallas_call | solution.py:253
  419.8 10.6 %collective-permute-done.27 = bf16[1024,576]{0,1:T(8,128)(2,1)} collective-permute-done((bf16[1024,576]{0,1:T(8,128)(2,1)S(1)}, bf16[1024,576]{0,1:T(8,128)(2,1)}, u32[]{:S(2)}, u32[]{:S(2)}) %collective-permute-start.27) | collective-permute-done | bytes 1179680 | tf_op jit(solution)/shard_map/ppermute | solution.py:492
  447.3 10.8 %collective-permute-done.30 = bf16[256,2048]{1,0:T(8,128)(2,1)} collective-permute-done((bf16[256,2048]{1,0:T(8,128)(2,1)}, bf16[256,2048]{1,0:T(8,128)(2,1)}, u32[]{:S(2)}, u32[]{:S(2)}) %collective-permute-start.30) | collective-permute-done | bytes 1048608 | tf_op jit(solution)/shard_map/ppermute | solution.py:492
  459.9 10.1 %all-to-all-done.4.in_ref = bf16[4,4,64,576]{3,2,1,0:T(8,128)(2,1)S(1)} async-done(((bf16[4,4,64,576]{3,2,1,0:T(8,128)(2,1)}), bf16[4,4,64,576]{3,2,1,0:T(8,128)(2,1)S(1)}, u32[]{:S(2)}, u32[]{:S(2)}) %all-to-all-start.4) | async-done | bytes 1179680 | tf_op jit(solution)/shard_map/all_to_all | solution.py:740
  (480 shorter events, 283.9 us)
Async XLA Ops:
  11.4 46.3 %all-to-all-start = ((bf16[4,104,2048]{2,1,0:T(8,128)(2,1)}), bf16[4,104,2048]{2,1,0:T(8,128)(2,1)}, u32[]{:S(2)}, u32[]{:S(2)}) async-start(bf16[4,104,2048]{2,1,0:T(8,128)(2,1)} %broadcast_in_dim.21), calls=%async_computation | async-start | bytes 3407872 | tf_op jit(solution)/shard_map/all_to_all | solution.py:553
  17.8 197.6 %all-gather.6.cloned.1.call-start = ((), (), s32[]{:S(2)}) async-start(), calls=%async_computation.10 | async-start | bytes 6488064 | tf_op jit(solution)/shard_map/all_gather | solution.py:569
  26.7 27.6 %collective-permute-start.2 = (bf16[256,2048]{1,0:T(8,128)(2,1)}, bf16[256,2048]{1,0:T(8,128)(2,1)}, u32[]{:S(2)}, u32[]{:S(2)}) collective-permute-start(bf16[256,2048]{1,0:T(8,128)(2,1)} %fusion.22), channel_id=1, source_target_pairs={{0,4},{1,5},{2,6},{3,7},{4,0},{5,1},{6,2},{7,3},{8,12},{9,13},{10,... | collective-permute-start | bytes 3145736 | tf_op jit(solution)/shard_map/ppermute | solution.py:492
  63.7 29.5 %collective-permute-start.3 = (bf16[256,2048]{1,0:T(8,128)(2,1)S(1)}, bf16[256,2048]{1,0:T(8,128)(2,1)}, u32[]{:S(2)}, u32[]{:S(2)}) collective-permute-start(bf16[256,2048]{1,0:T(8,128)(2,1)S(1)} %block_order.6), channel_id=1, source_target_pairs={{0,1},{1,0},{2,3},{3,2},{4,5},{5,4},{6,7},{7,6},{8,9},{9,8},{10,11... | collective-permute-start | bytes 3145736 | tf_op jit(solution)/shard_map/ppermute | solution.py:492
  64.7 28.5 %collective-permute-start.4 = (bf16[256,2048]{1,0:T(8,128)(2,1)}, bf16[256,2048]{1,0:T(8,128)(2,1)}, u32[]{:S(2)}, u32[]{:S(2)}) collective-permute-start(bf16[256,2048]{1,0:T(8,128)(2,1)} %collective-permute-done), channel_id=1, source_target_pairs={{0,1},{1,0},{2,3},{3,2},{4,5},{5,4},{6,7},{7,6},{8,9},{9,8},{10,11... | collective-permute-start | bytes 3145736 | tf_op jit(solution)/shard_map/ppermute | solution.py:492
  75.9 150.4 %all-gather.8.cloned.1.call-start = ((), (), s32[]{:S(2)}) async-start(), calls=%async_computation.11 | async-start | bytes 6488064 | tf_op jit(solution)/shard_map/all_gather | solution.py:584
  93.3 164.6 %all-gather.4.cloned.1.call-start = ((), (), s32[]{:S(2)}) async-start(), calls=%async_computation.9 | async-start | bytes 6488064 | tf_op jit(solution)/shard_map/all_gather | solution.py:625
  107.6 30.5 %collective-permute-start.10 = (bf16[4,4,64,576]{3,2,1,0:T(8,128)(2,1)}, bf16[4,4,64,576]{3,2,1,0:T(8,128)(2,1)}, u32[]{:S(2)}, u32[]{:S(2)}) collective-permute-start(bf16[4,4,64,576]{3,2,1,0:T(8,128)(2,1)} %all-to-all-done.1), channel_id=1, source_target_pairs={{0,4},{1,5},{2,6},{3,7},{4,0},{5,1},{6,2},{7,3},{8,12},{9,13},{10,... | collective-permute-start | bytes 3538952 | tf_op jit(solution)/shard_map/ppermute | solution.py:492
  133.7 28.9 %collective-permute-start.13 = (bf16[2,4,40,2048]{3,2,1,0:T(8,128)(2,1)S(1)}, bf16[2,4,40,2048]{3,2,1,0:T(8,128)(2,1)}, u32[]{:S(2)}, u32[]{:S(2)}) collective-permute-start(bf16[2,4,40,2048]{3,2,1,0:T(8,128)(2,1)S(1)} %copy-done.58), channel_id=1, source_target_pairs={{0,2},{1,3},{2,0},{3,1},{4,6},{5,7},{6,4},{7,5},{8,10},{9,11},{10,... | collective-permute-start | bytes 3932168 | tf_op jit(solution)/shard_map/ppermute | solution.py:492
  178.1 156.9 %reduce-scatter.4.cloned.1.call-start = ((), (), s32[]{:S(2)}) async-start(), calls=%async_computation.12 | async-start | bytes 6488064 | tf_op jit(solution)/shard_map/reduce_scatter | solution.py:649
  189.6 49.0 %collective-permute-start.19 = (bf16[256,2048]{1,0:T(8,128)(2,1)S(1)}, bf16[256,2048]{1,0:T(8,128)(2,1)S(1)}, u32[]{:S(2)}, u32[]{:S(2)}) collective-permute-start(bf16[256,2048]{1,0:T(8,128)(2,1)S(1)} %multiply_convert_fusion.3), channel_id=1, source_target_pairs={{0,6},{1,7},{2,4},{3,5},{4,2},{5,3},{6,0},{7,1},{8,14},{9,15},{10,... | collective-permute-start | bytes 3145736 | tf_op jit(solution)/shard_map/ppermute | solution.py:492
  257.9 141.7 %reduce-scatter.6.cloned.1.call-start = ((), (), s32[]{:S(2)}) async-start(), calls=%async_computation.13 | async-start | bytes 6488064 | tf_op jit(solution)/shard_map/reduce_scatter | solution.py:649
  307.2 164.8 %reduce-scatter.8.cloned.1.call-start = ((), (), s32[]{:S(2)}) async-start(), calls=%async_computation.14 | async-start | bytes 6488064 | tf_op jit(solution)/shard_map/reduce_scatter | solution.py:649
  308.7 26.3 %collective-permute-start.21 = (bf16[256,2048]{1,0:T(8,128)(2,1)}, bf16[256,2048]{1,0:T(8,128)(2,1)}, u32[]{:S(2)}, u32[]{:S(2)}) collective-permute-start(bf16[256,2048]{1,0:T(8,128)(2,1)} %get-tuple-element.223), channel_id=1, source_target_pairs={{0,4},{1,5},{2,6},{3,7},{4,0},{5,1},{6,2},{7,3},{8,12},{9,13},{10,... | collective-permute-start | bytes 3145736 | tf_op jit(solution)/shard_map/ppermute | solution.py:492
  352.2 47.4 %collective-permute-start.25 = (bf16[256,2048]{1,0:T(8,128)(2,1)}, bf16[256,2048]{1,0:T(8,128)(2,1)}, u32[]{:S(2)}, u32[]{:S(2)}) collective-permute-start(bf16[256,2048]{1,0:T(8,128)(2,1)} %slice.112), channel_id=1, source_target_pairs={{0,4},{1,5},{2,6},{3,7},{4,0},{5,1},{6,2},{7,3},{8,12},{9,13},{10,... | collective-permute-start | bytes 3145736 | tf_op jit(solution)/shard_map/ppermute | solution.py:492
  352.5 47.5 %collective-permute-start.26 = (bf16[256,2048]{1,0:T(8,128)(2,1)}, bf16[256,2048]{1,0:T(8,128)(2,1)}, u32[]{:S(2)}, u32[]{:S(2)}) collective-permute-start(bf16[256,2048]{1,0:T(8,128)(2,1)} %convolution_convert_fusion.4), channel_id=1, source_target_pairs={{0,4},{1,5},{2,6},{3,7},{4,0},{5,1},{6,2},{7,3},{8,12},{9,13},{10,... | collective-permute-start | bytes 3145736 | tf_op jit(solution)/shard_map/ppermute | solution.py:492
  403.3 27.1 %collective-permute-start.27 = (bf16[1024,576]{0,1:T(8,128)(2,1)S(1)}, bf16[1024,576]{0,1:T(8,128)(2,1)}, u32[]{:S(2)}, u32[]{:S(2)}) collective-permute-start(bf16[1024,576]{0,1:T(8,128)(2,1)S(1)} %fusion.23), channel_id=1, source_target_pairs={{0,4},{1,5},{2,6},{3,7},{4,0},{5,1},{6,2},{7,3},{8,12},{9,13},{10,... | collective-permute-start | bytes 3538952 | tf_op jit(solution)/shard_map/ppermute | solution.py:492
  403.6 35.8 %collective-permute-start.32 = (bf16[320,2048]{1,0:T(8,128)(2,1)}, bf16[320,2048]{1,0:T(8,128)(2,1)}, u32[]{:S(2)}, u32[]{:S(2)}) collective-permute-start(bf16[320,2048]{1,0:T(8,128)(2,1)} %add_convert_fusion.5), channel_id=1, source_target_pairs={{0,2},{1,3},{2,0},{3,1},{4,6},{5,7},{6,4},{7,5},{8,10},{9,11},{10,... | collective-permute-start | bytes 3932168 | tf_op jit(solution)/shard_map/ppermute | solution.py:492
  410.2 61.8 %collective-permute-start.31 = (bf16[2,256,2048]{2,1,0:T(8,128)(2,1)}, bf16[2,256,2048]{2,1,0:T(8,128)(2,1)}, u32[]{:S(2)}, u32[]{:S(2)}) collective-permute-start(bf16[2,256,2048]{2,1,0:T(8,128)(2,1)} %dynamic-slice_bitcast_fusion), channel_id=1, source_target_pairs={{0,1},{1,0},{2,3},{3,2},{4,5},{5,4},{6,7},{7,6},{8,9},{9,8},{10,11... | collective-permute-start | bytes 6291464 | tf_op jit(solution)/shard_map/ppermute | solution.py:492
  418.8 39.4 %collective-permute-start.30 = (bf16[256,2048]{1,0:T(8,128)(2,1)}, bf16[256,2048]{1,0:T(8,128)(2,1)}, u32[]{:S(2)}, u32[]{:S(2)}) collective-permute-start(bf16[256,2048]{1,0:T(8,128)(2,1)} %fusion.14), channel_id=1, source_target_pairs={{0,2},{1,3},{2,0},{3,1},{4,6},{5,7},{6,4},{7,5},{8,10},{9,11},{10,... | collective-permute-start | bytes 3145736 | tf_op jit(solution)/shard_map/ppermute | solution.py:492
  434.3 35.6 %all-to-all-start.4 = ((bf16[4,4,64,576]{3,2,1,0:T(8,128)(2,1)}), bf16[4,4,64,576]{3,2,1,0:T(8,128)(2,1)S(1)}, u32[]{:S(2)}, u32[]{:S(2)}) async-start(bf16[4,4,64,576]{3,2,1,0:T(8,128)(2,1)} %bitcast.189), calls=%async_computation.6 | async-start | bytes 2621440 | tf_op jit(solution)/shard_map/all_to_all | solution.py:740
  442.8 34.8 %collective-permute-start.34 = (bf16[4,40,2048]{2,1,0:T(8,128)(2,1)}, bf16[4,40,2048]{2,1,0:T(8,128)(2,1)}, u32[]{:S(2)}, u32[]{:S(2)}) collective-permute-start(bf16[4,40,2048]{2,1,0:T(8,128)(2,1)} %bitcast.49), channel_id=1, source_target_pairs={{0,4},{1,5},{2,6},{3,7},{4,0},{5,1},{6,2},{7,3},{8,12},{9,13},{10,... | collective-permute-start | bytes 1966088 | tf_op jit(solution)/shard_map/ppermute | solution.py:492
  487.6 41.8 %collective-permute-start.44 = (bf16[256,1408]{1,0:T(8,128)(2,1)}, bf16[256,1408]{1,0:T(8,128)(2,1)}, u32[]{:S(2)}, u32[]{:S(2)}) collective-permute-start(bf16[256,1408]{1,0:T(8,128)(2,1)} %reduce-scatter.8.cloned.1.call-done.own_ref), channel_id=1, source_target_pairs={{1,4},{3,6},{4,1},{6,3},{9,12},{11,14},{12,9},{14,11},{17,20},{19,... | collective-permute-start | bytes 2162696 | tf_op jit(solution)/shard_map/ppermute | solution.py:492
  489.3 47.5 %all-to-all-start.5 = ((bf16[4,64,1920]{2,1,0:T(8,128)(2,1)}), bf16[4,64,1920]{2,1,0:T(8,128)(2,1)}, u32[]{:S(2)}, u32[]{:S(2)}) async-start(bf16[4,64,1920]{2,1,0:T(8,128)(2,1)} %join_columns.1), calls=%async_computation.8 | async-start | bytes 1966080 | tf_op jit(solution)/shard_map/all_to_all | solution.py:750
  (145 other events, 1390.2 us)
Sparse Core Ops, SparseCore 0:
  57.8 59.5 all-gather.5
  119.6 59.0 all-gather.7
  180.4 59.1 all-gather.3
  258.0 62.0 reduce-scatter.3
  322.2 63.2 reduce-scatter.5
  387.6 63.2 reduce-scatter.7
where the time goes:
time: 554 us; the launch traced here: 549 us
  matrix products  143 us (26%)
  waiting for transfers between devices  133 us (24%)
  other arithmetic  78.2 us (14%)
  starting transfers between devices  71.7 us (13%)
  local copies, waits for them, and re-layouts  46.1 us (8%)
  Pallas kernels  45.2 us (8%)
  between operations  17.5 us (3%)
  blocking collectives  13.7 us (2%)
    dot_general x35, matrix products, contract(): lax.dot_general(left, right, (((left_dim,), (right_dim,)), ((), ())), pre...  143 us
    ppermute x45, waiting for transfers between devices, permute(): lax.ppermute(array, ALL, [pair for pair in pairs if pair[0] != pair[1]])  103 us
    ppermute x45, starting transfers between devices, permute(): lax.ppermute(array, ALL, [pair for pair in pairs if pair[0] != pair[1]])  48.2 us
    unnamed x229, local copies, waits for them, and re-layouts  23.2 us
    pallas_call x1, Pallas kernels, attend_back(): pl.pallas_call(functools.partial(backward_kernel, block=block), name='att...  15.8 us
    all_to_all x1, blocking collectives, local(): lax.all_to_all(outgoing, KV, split_axis=0, concat_axis=0, tiled=True)  13.7 us
    all_to_all x1, waiting for transfers between devices, local(): lax.all_to_all(qkv_parts, KV, split_axis=0, concat_axis=0, tiled=True)  12.7 us
    pallas_call x3, Pallas kernels, adamw_block(): pl.pallas_call(functools.partial(adamw_kernel, rate=rate, shrink=shrink),...  12 us
  transfers between devices with their start and end apart: 56, of which 21 were waited for; matrix products, arithmetic and copies ran while one was open for 43% of the time, Pallas kernels for 8%

commit v1 on v0

--- a/solution.py
+++ b/solution.py
@@ -606,7 +606,9 @@
     normed, qkv_rows = stage(normed, qkv_rows)
     qkv_full = jnp.concatenate([qkv_rows, qkv_far]).reshape(model, span)
 
-    mixed = contract(qkv_full, normed, 0, 1)
+    mixed = contract(qkv_rows.reshape(-1, span), normed[:, : model // 2], 0, 1)
+    mixed = lax.optimization_barrier(mixed)
+    mixed = mixed + contract(qkv_far.reshape(-1, span), normed[:, model // 2 :], 0, 1)
     query_rows, key_rows, value_rows, outgoing, lse = attend(
         groups, mixed, cosine, sine, gain_q, gain_k, heads, item_count
     )
@@ -751,11 +753,6 @@
     grad_normed = lax.dynamic_index_in_dim(grad_normed, core, 1, keepdims=False).astype(high)
     grad_normed = (grad_normed + normed_moved.astype(high)).astype(low)
     grad_normed = halve(grad_normed, lax.axis_index("kh"), 0, lambda v: in_sequence(v, 2)).astype(high)
-    steps_done = step_count[0].astype(high)
-    fixes = jnp.stack(
-        [1.0 - jnp.power(beta_first, steps_done), 1.0 - jnp.power(beta_second, steps_done)]
-    )
-    grad_normed, fixes = stage(grad_normed, fixes)
     line = lax.axis_index("sh")
 
     def sum_line(blocks):
@@ -796,12 +793,16 @@
     grad_gains = grad_gains[0] + in_sequence(grad_gains[1], 2)
     gains_grad = sum_line(grad_gains.reshape(z_size, -1))
 
+    steps_done = step_count[0].astype(high)
     new_qkv, moments_qkv = adamw(qkv_weight, qkv_grad, first_qkv, second_qkv, 0.02, 0.1, steps_done)
     new_out, moments_out = adamw(out_weight, out_grad, first_out, second_out, 0.2, 0.1, steps_done)
     new_gains, moments_gains = adamw(
         gains, gains_grad, first_gains, second_gains, 0.6, 0.0, steps_done
     )
     stays = (lax.axis_index("sl") == lax.axis_index("kl")).astype(jnp.int32)
+    fixes = jnp.stack(
+        [1.0 - jnp.power(beta_first, steps_done), 1.0 - jnp.power(beta_second, steps_done)]
+    )
     new_gate, moments_gate = adamw_block(
         gate_weight, grad_gate_w, first_gate, second_gate, 0.02, 0.1, stays, fixes
     )

time: 554 us -> 561 us (1.013); the launches traced: 549 us -> 549 us
  local copies, waits for them, and re-layouts: 46.1 us -> 38 us
  matrix products: 143 us -> 150 us
    dot_general x35 -> x36, matrix products: 143 us -> 150 us  [contract(): lax.dot_general(left, right, (((left_dim,), (right_dim,)), ((), ())), pre...]
    unnamed x229 -> x227, local copies, waits for them, and re-layouts: 23.2 us -> 18.5 us
  transfers between devices with their start and end apart: 56 -> 56, of which waited for: 21 -> 19; matrix products, arithmetic and copies ran while one was open for 43% -> 43% of each run, Pallas kernels for 8% -> 9%
where the time goes in v1:
time: 561 us; the launch traced here: 549 us
  matrix products  150 us (27%)
  waiting for transfers between devices  134 us (24%)
  other arithmetic  77.1 us (14%)
  starting transfers between devices  71.4 us (13%)
  Pallas kernels  47.4 us (8%)
  local copies, waits for them, and re-layouts  38 us (7%)
  between operations  18.1 us (3%)
  blocking collectives  13.6 us (2%)
    dot_general x36, matrix products, contract(): lax.dot_general(left, right, (((left_dim,), (right_dim,)), ((), ())), pre...  150 us
    ppermute x45, waiting for transfers between devices, permute(): lax.ppermute(array, ALL, [pair for pair in pairs if pair[0] != pair[1]])  101 us
    ppermute x45, starting transfers between devices, permute(): lax.ppermute(array, ALL, [pair for pair in pairs if pair[0] != pair[1]])  48.1 us
    unnamed x227, local copies, waits for them, and re-layouts  18.5 us
    pallas_call x1, Pallas kernels, attend_back(): pl.pallas_call(functools.partial(backward_kernel, block=block), name='att...  15.8 us
    pallas_call x3, Pallas kernels, adamw_block(): pl.pallas_call(functools.partial(adamw_kernel, rate=rate, shrink=shrink),...  14.1 us
    all_to_all x1, blocking collectives, local(): lax.all_to_all(outgoing, KV, split_axis=0, concat_axis=0, tiled=True)  13.6 us
    all_to_all x1, waiting for transfers between devices, local(): lax.all_to_all(qkv_parts, KV, split_axis=0, concat_axis=0, tiled=True)  12.7 us
  transfers between devices with their start and end apart: 56, of which 19 were waited for; matrix products, arithmetic and copies ran while one was open for 43% of the time, Pallas kernels for 9%

profile of v1, /device:TPU:0, one launch (start us, length us, event | category | flops | bytes accessed | tf_op | source)
XLA Modules:
  0.0 549.5 jit_solution(10283995304454927521)
XLA Ops:
  11.4 6.4 %all-to-all-start = ((bf16[4,104,2048]{2,1,0:T(8,128)(2,1)}), bf16[4,104,2048]{2,1,0:T(8,128)(2,1)}, u32[]{:S(2)}, u32[]{:S(2)}) async-start(bf16[4,104,2048]{2,1,0:T(8,128)(2,1)} %broadcast_in_dim.21), calls=%async_computation | async-start | bytes 3407872 | tf_op jit(solution)/shard_map/all_to_all | solution.py:553
  31.8 14.0 %collective-permute-done = bf16[256,2048]{1,0:T(8,128)(2,1)} collective-permute-done((bf16[256,2048]{1,0:T(8,128)(2,1)S(1)}, bf16[256,2048]{1,0:T(8,128)(2,1)}, u32[]{:S(2)}, u32[]{:S(2)}) %collective-permute-start) | collective-permute-done | bytes 1048608 | tf_op jit(solution)/shard_map/ppermute | solution.py:492
  45.8 8.4 %collective-permute-done.2 = bf16[256,2048]{1,0:T(8,128)(2,1)} collective-permute-done((bf16[256,2048]{1,0:T(8,128)(2,1)}, bf16[256,2048]{1,0:T(8,128)(2,1)}, u32[]{:S(2)}, u32[]{:S(2)}) %collective-permute-start.2) | collective-permute-done | bytes 1048608 | tf_op jit(solution)/shard_map/ppermute | solution.py:492
  80.5 12.7 %all-to-all-done.1 = bf16[4,4,64,576]{3,2,1,0:T(8,128)(2,1)} async-done(((bf16[4,4,64,576]{3,2,1,0:T(8,128)(2,1)}), bf16[4,4,64,576]{3,2,1,0:T(8,128)(2,1)}, u32[]{:S(2)}, u32[]{:S(2)}) %all-to-all-start.1) | async-done | bytes 1179680 | tf_op jit(solution)/shard_map/all_to_all | solution.py:575
  107.5 20.0 %collective-permute-done.11 = bf16[256,2048]{1,0:T(8,128)(2,1)} collective-permute-done((bf16[256,2048]{1,0:T(8,128)(2,1)}, bf16[256,2048]{1,0:T(8,128)(2,1)}, u32[]{:S(2)}, u32[]{:S(2)}) %collective-permute-start.11) | collective-permute-done | bytes 1048608 | tf_op jit(solution)/shard_map/ppermute | solution.py:492
  141.0 10.4 %attention_forward.1 = (bf16[5,64,1024]{2,1,0:T(8,128)(2,1)S(1)}, bf16[2,64,1024]{2,1,0:T(8,128)(2,1)S(1)}, bf16[2,64,1024]{2,1,0:T(8,128)(2,1)S(1)}, bf16[4,320,256]{2,1,0:T(8,128)(2,1)S(1)}, f32[5,1,1024]{2,1,0:T(1,128)S(1)}) custom-call(s32[5]{0:T(128)S(1)} %and_select_fusion.group_ref, f32[576,1024]{1,0:T(8,128)S(1)} %fusion.26.qp_ref.kp_ref.vp_ref, ...), custom_call_target="tpu_custom_call" | custom-call | flops 671088640 | bytes 8000000 | tf_op jit(solution)/shard_map/attention_forward/pallas_call | solution.py:221
  157.6 13.6 %all_to_all.30 = bf16[4,320,256]{2,1,0:T(8,128)(2,1)S(1)} all-to-all(bf16[4,320,256]{2,1,0:T(8,128)(2,1)S(1)} %get-tuple-element.126), channel_id=1, replica_groups=mesh['sh'=4,'sl'=2,'kh'=2,'kl'=2] {'kh','kl'}, dimensions={0} | all-to-all | bytes 1310720 | tf_op jit(solution)/shard_map/all_to_all | solution.py:621
  185.1 21.7 %collective-permute-done.17 = bf16[256,2048]{1,0:T(8,128)(2,1)S(1)} collective-permute-done((bf16[256,2048]{1,0:T(8,128)(2,1)S(1)}, bf16[256,2048]{1,0:T(8,128)(2,1)S(1)}, u32[]{:S(2)}, u32[]{:S(2)}) %collective-permute-start.17) | collective-permute-done | bytes 1048608 | tf_op jit(solution)/shard_map/ppermute | solution.py:492
  209.7 10.6 %fusion.69 = f32[768,1408]{1,0:T(8,128)} fusion(bf16[2048,1408]{1,0:T(8,128)(2,1)} %all-gather.6.cloned.1.call-done, bf16[256,2048]{1,0:T(8,128)(2,1)} %collective-permute-done.18, bf16[256,2048]{1,0:T(8,128)(2,1)S(1)} %collective-permute-done.17, bf16[256,2048]{1,0:T(8,128)(2,1)S(1)} %multiply_convert_fusion.3), kind=kOutput, calls=%fused_computation.176 | convolution fusion | flops 4438622208 | bytes 13238272 | tf_op jit(solution)/shard_map/dot_general | solution.py:49
  220.3 12.3 %multiply_convert_fusion.2 = (bf16[768,1408]{1,0:T(8,128)(2,1)S(1)}, f32[768,1408]{1,0:T(8,128)}, f32[768,1408]{1,0:T(8,128)}) fusion(f32[768,1408]{1,0:T(8,128)} %fusion.69, bf16[2048,1408]{1,0:T(8,128)(2,1)} %all-gather.8.cloned.1.call-done, bf16[256,2048]{1,0:T(8,128)(2,1)} %collective-permute-done.18, ...), kind=kOutput, calls=%fused_computation.10 | convolution fusion | flops 4445110272 | bytes 24051712 | tf_op jit(solution)/shard_map/dot_general | solution.py:49
  239.9 7.0 %fusion.67 = f32[2048,1408]{1,0:T(8,128)S(1)} fusion(bf16[768,1408]{1,0:T(8,128)(2,1)S(1)} %get-tuple-element.143, bf16[256,2048]{1,0:T(8,128)(2,1)} %multiply_convert_fusion.4, bf16[256,2048]{1,0:T(8,128)(2,1)} %collective-permute-done.2, bf16[256,2048]{1,0:T(8,128)(2,1)} %fusion.17), kind=kOutput, calls=%fused_computation.174 | convolution fusion | flops 4438622208 | bytes 16842752 | tf_op jit(solution)/shard_map/dot_general | solution.py:49
  246.9 5.5 %add_convert_fusion.2 = bf16[2048,1408]{1,0:T(8,128)(2,1)} fusion(f32[2048,1408]{1,0:T(8,128)S(1)} %fusion.67, bf16[256,2048]{1,0:T(8,128)(2,1)} %collective-permute-done.12, bf16[256,1408]{1,0:T(8,128)(2,1)S(1)} %get-tuple-element.252), kind=kOutput, calls=%fused_computation.2 | convolution fusion | flops 1482162176 | bytes 19070976 | tf_op jit(solution)/shard_map/dot_general | solution.py:49
  254.9 7.1 %multiply_convert_fusion.5 = (bf16[256,1408]{1,0:T(8,128)(2,1)S(1)}, bf16[256,1408]{1,0:T(8,128)(2,1)S(1)}) fusion(f32[256,1408]{1,0:T(8,128)} %copy-done.95, f32[256,1408]{1,0:T(8,128)} %get-tuple-element.253, bf16[256,2048]{1,0:T(8,128)(2,1)} %collective-permute-done.12, bf16[2048,1408]{1,0:T(8,128)(2,1)} %all-gather.4.cloned.1.call-done), kind=kOutput, calls=%fused_computation.72 | convolution fusion | flops 1481080832 | bytes 11141120 | tf_op jit(solution)/shard_map/dot_general | solution.py:49
  266.7 8.4 %fusion.81 = f32[768,1408]{1,0:T(8,128)S(1)} fusion(bf16[768,2048]{1,0:T(8,128)(2,1)S(1)} %pad_maximum_fusion, bf16[2048,1408]{1,0:T(8,128)(2,1)} %all-gather.4.cloned.1.call-done), kind=kOutput, calls=%fused_computation.186 | convolution fusion | flops 4429185024 | bytes 13238272 | tf_op jit(solution)/shard_map/dot_general | solution.py:49
  281.8 8.5 %add_convert_fusion.3 = bf16[768,2048]{1,0:T(8,128)(2,1)S(1)} fusion(f32[768,2048]{1,0:T(8,128)S(1)} %fusion.82, bf16[768,1408]{1,0:T(8,128)(2,1)S(1)} %get-tuple-element.154, bf16[2048,1408]{1,0:T(8,128)(2,1)} %all-gather.8.cloned.1.call-done), kind=kOutput, calls=%fused_computation.7 | convolution fusion | flops 4432330752 | bytes 17367040 | tf_op jit(solution)/shard_map/dot_general | solution.py:49
  292.9 8.7 %add_convert_fusion = bf16[2048,1408]{1,0:T(8,128)(2,1)} fusion(f32[2048,1408]{1,0:T(8,128)S(1)} %fusion.84, bf16[768,1408]{1,0:T(8,128)(2,1)S(1)} %get-tuple-element.166, bf16[256,2048]{1,0:T(8,128)(2,1)} %collective-permute-done.18, bf16[256,2048]{1,0:T(8,128)(2,1)S(1)} %copy-done.92, bf16[256,2048]{1,0:T(8,128)(2,1)S(1)} %copy-done.69), kind=kOutput, calls=%fused_computation | convolution fusion | flops 4444389376 | bytes 22609920 | tf_op jit(solution)/shard_map/dot_general | solution.py:49
  305.8 5.4 convolution_convert_fusion.4
  311.3 6.7 %convolution_convert_fusion.1 = bf16[768,2048]{1,0:T(8,128)(2,1)} fusion(bf16[768,1408]{1,0:T(8,128)(2,1)S(1)} %copy-done.97, bf16[2048,1408]{1,0:T(8,128)(2,1)S(1)} %bitcast.233), kind=kOutput, calls=%fused_computation.15 | convolution fusion | flops 4430757888 | bytes 11075584 | tf_op jit(solution)/shard_map/dot_general | solution.py:49
  320.2 9.2 %add_convert_fusion.1 = bf16[2048,1408]{1,0:T(8,128)(2,1)} fusion(f32[2048,1408]{1,0:T(8,128)S(1)} %fusion.83, bf16[768,1408]{1,0:T(8,128)(2,1)S(1)} %copy-done.65, bf16[256,2048]{1,0:T(8,128)(2,1)} %collective-permute-done.18, bf16[256,2048]{1,0:T(8,128)(2,1)S(1)} %copy-done.93, bf16[256,2048]{1,0:T(8,128)(2,1)S(1)} %copy-done.70), kind=kOutput, calls=%fused_computation.1 | convolution fusion | flops 4444389376 | bytes 22609920 | tf_op jit(solution)/shard_map/dot_general | solution.py:49
  338.5 5.7 %fusion.72 = (bf16[256,2048]{1,0:T(8,128)(2,1)S(1)}, f32[256,2048]{1,0:T(8,128)}) fusion(f32[256]{0:T(256)S(1)} %broadcast_multiply_fusion.1, f32[256,2048]{1,0:T(8,128)S(1)} %copy-done.42, f32[2048]{0:T(1024)S(1)} %copy-done.80, bf16[256,2048]{1,0:T(8,128)(2,1)} %collective-permute-done.20, bf16[256,2048]{1,0:T(8,128)(2,1)} %copy-done.59, ...), kind=kLoop, calls=%fused_computation.177 | loop fusion | flops 8388608 | bytes 10496004 | tf_op jit(solution)/shard_map/convert_element_type | solution.py:687
  380.2 15.8 %attention_backward.1 = (bf16[320,1024]{1,0:T(8,128)(2,1)S(1)}, bf16[2,64,1024]{2,1,0:T(8,128)(2,1)S(1)}, bf16[2,64,1024]{2,1,0:T(8,128)(2,1)S(1)}, f32[64,1]{1,0:T(8,128)S(1)}, f32[64,1]{1,0:T(8,128)S(1)}) custom-call(s32[5]{0:T(128)S(1)} %copy-done.40, f32[576,1024]{1,0:T(8,128)S(1)} %copy-done.1, f32[576,1024]{1,0:T(8,128)S(1)} %copy-done.1, ...), custom_call_target="tpu_custom_call" | custom-call | flops 1677721600 | bytes 10000000 | tf_op jit(solution)/shard_map/attention_backward/pallas_call | solution.py:253
  417.9 11.6 %collective-permute-done.27 = bf16[1024,576]{0,1:T(8,128)(2,1)} collective-permute-done((bf16[1024,576]{0,1:T(8,128)(2,1)}, bf16[1024,576]{0,1:T(8,128)(2,1)}, u32[]{:S(2)}, u32[]{:S(2)}) %collective-permute-start.27) | collective-permute-done | bytes 1179680 | tf_op jit(solution)/shard_map/ppermute | solution.py:492
  446.5 10.5 %collective-permute-done.30 = bf16[256,2048]{1,0:T(8,128)(2,1)} collective-permute-done((bf16[256,2048]{1,0:T(8,128)(2,1)}, bf16[256,2048]{1,0:T(8,128)(2,1)}, u32[]{:S(2)}, u32[]{:S(2)}) %collective-permute-start.30) | collective-permute-done | bytes 1048608 | tf_op jit(solution)/shard_map/ppermute | solution.py:492
  457.0 11.9 %all-to-all-done.4.in_ref = bf16[4,4,64,576]{3,2,1,0:T(8,128)(2,1)S(1)} async-done(((bf16[4,4,64,576]{3,2,1,0:T(8,128)(2,1)}), bf16[4,4,64,576]{3,2,1,0:T(8,128)(2,1)S(1)}, u32[]{:S(2)}, u32[]{:S(2)}) %all-to-all-start.4) | async-done | bytes 1179680 | tf_op jit(solution)/shard_map/all_to_all | solution.py:742
  (478 shorter events, 279.1 us)
Async XLA Ops:
  11.4 46.3 %all-to-all-start = ((bf16[4,104,2048]{2,1,0:T(8,128)(2,1)}), bf16[4,104,2048]{2,1,0:T(8,128)(2,1)}, u32[]{:S(2)}, u32[]{:S(2)}) async-start(bf16[4,104,2048]{2,1,0:T(8,128)(2,1)} %broadcast_in_dim.21), calls=%async_computation | async-start | bytes 3407872 | tf_op jit(solution)/shard_map/all_to_all | solution.py:553
  17.8 191.9 %all-gather.6.cloned.1.call-start = ((), (), s32[]{:S(2)}) async-start(), calls=%async_computation.10 | async-start | bytes 6488064 | tf_op jit(solution)/shard_map/all_gather | solution.py:569
  26.6 27.6 %collective-permute-start.2 = (bf16[256,2048]{1,0:T(8,128)(2,1)}, bf16[256,2048]{1,0:T(8,128)(2,1)}, u32[]{:S(2)}, u32[]{:S(2)}) collective-permute-start(bf16[256,2048]{1,0:T(8,128)(2,1)} %fusion.17), channel_id=1, source_target_pairs={{0,4},{1,5},{2,6},{3,7},{4,0},{5,1},{6,2},{7,3},{8,12},{9,13},{10,... | collective-permute-start | bytes 3145736 | tf_op jit(solution)/shard_map/ppermute | solution.py:492
  63.7 29.6 %collective-permute-start.3 = (bf16[256,2048]{1,0:T(8,128)(2,1)S(1)}, bf16[256,2048]{1,0:T(8,128)(2,1)}, u32[]{:S(2)}, u32[]{:S(2)}) collective-permute-start(bf16[256,2048]{1,0:T(8,128)(2,1)S(1)} %block_order.6), channel_id=1, source_target_pairs={{0,1},{1,0},{2,3},{3,2},{4,5},{5,4},{6,7},{7,6},{8,9},{9,8},{10,11... | collective-permute-start | bytes 3145736 | tf_op jit(solution)/shard_map/ppermute | solution.py:492
  64.7 28.5 %collective-permute-start.4 = (bf16[256,2048]{1,0:T(8,128)(2,1)}, bf16[256,2048]{1,0:T(8,128)(2,1)}, u32[]{:S(2)}, u32[]{:S(2)}) collective-permute-start(bf16[256,2048]{1,0:T(8,128)(2,1)} %collective-permute-done), channel_id=1, source_target_pairs={{0,1},{1,0},{2,3},{3,2},{4,5},{5,4},{6,7},{7,6},{8,9},{9,8},{10,11... | collective-permute-start | bytes 3145736 | tf_op jit(solution)/shard_map/ppermute | solution.py:492
  75.9 144.4 %all-gather.8.cloned.1.call-start = ((), (), s32[]{:S(2)}) async-start(), calls=%async_computation.11 | async-start | bytes 6488064 | tf_op jit(solution)/shard_map/all_gather | solution.py:584
  93.3 159.2 %all-gather.4.cloned.1.call-start = ((), (), s32[]{:S(2)}) async-start(), calls=%async_computation.9 | async-start | bytes 6488064 | tf_op jit(solution)/shard_map/all_gather | solution.py:627
  101.3 35.1 %collective-permute-start.10 = (bf16[4,4,64,576]{3,2,1,0:T(8,128)(2,1)}, bf16[4,4,64,576]{3,2,1,0:T(8,128)(2,1)}, u32[]{:S(2)}, u32[]{:S(2)}) collective-permute-start(bf16[4,4,64,576]{3,2,1,0:T(8,128)(2,1)} %all-to-all-done.1), channel_id=1, source_target_pairs={{0,4},{1,5},{2,6},{3,7},{4,0},{5,1},{6,2},{7,3},{8,12},{9,13},{10,... | collective-permute-start | bytes 3538952 | tf_op jit(solution)/shard_map/ppermute | solution.py:492
  127.6 28.9 %collective-permute-start.13 = (bf16[2,4,40,2048]{3,2,1,0:T(8,128)(2,1)S(1)}, bf16[2,4,40,2048]{3,2,1,0:T(8,128)(2,1)}, u32[]{:S(2)}, u32[]{:S(2)}) collective-permute-start(bf16[2,4,40,2048]{3,2,1,0:T(8,128)(2,1)S(1)} %copy-done.53), channel_id=1, source_target_pairs={{0,2},{1,3},{2,0},{3,1},{4,6},{5,7},{6,4},{7,5},{8,10},{9,11},{10,... | collective-permute-start | bytes 3932168 | tf_op jit(solution)/shard_map/ppermute | solution.py:492
  172.4 157.2 %reduce-scatter.4.cloned.1.call-start = ((), (), s32[]{:S(2)}) async-start(), calls=%async_computation.12 | async-start | bytes 6488064 | tf_op jit(solution)/shard_map/reduce_scatter | solution.py:651
  183.9 48.7 %collective-permute-start.19 = (bf16[256,2048]{1,0:T(8,128)(2,1)S(1)}, bf16[256,2048]{1,0:T(8,128)(2,1)S(1)}, u32[]{:S(2)}, u32[]{:S(2)}) collective-permute-start(bf16[256,2048]{1,0:T(8,128)(2,1)S(1)} %multiply_convert_fusion.3), channel_id=1, source_target_pairs={{0,6},{1,7},{2,4},{3,5},{4,2},{5,3},{6,0},{7,1},{8,14},{9,15},{10,... | collective-permute-start | bytes 3145736 | tf_op jit(solution)/shard_map/ppermute | solution.py:492
  252.5 144.8 %reduce-scatter.6.cloned.1.call-start = ((), (), s32[]{:S(2)}) async-start(), calls=%async_computation.13 | async-start | bytes 6488064 | tf_op jit(solution)/shard_map/reduce_scatter | solution.py:651
  301.6 169.3 %reduce-scatter.8.cloned.1.call-start = ((), (), s32[]{:S(2)}) async-start(), calls=%async_computation.14 | async-start | bytes 6488064 | tf_op jit(solution)/shard_map/reduce_scatter | solution.py:651
  303.2 26.3 %collective-permute-start.21 = (bf16[256,2048]{1,0:T(8,128)(2,1)}, bf16[256,2048]{1,0:T(8,128)(2,1)S(1)}, u32[]{:S(2)}, u32[]{:S(2)}) collective-permute-start(bf16[256,2048]{1,0:T(8,128)(2,1)} %get-tuple-element.220), channel_id=1, source_target_pairs={{0,4},{1,5},{2,6},{3,7},{4,0},{5,1},{6,2},{7,3},{8,12},{9,13},{10,... | collective-permute-start | bytes 3145736 | tf_op jit(solution)/shard_map/ppermute | solution.py:492
  350.2 47.2 %collective-permute-start.25 = (bf16[256,2048]{1,0:T(8,128)(2,1)}, bf16[256,2048]{1,0:T(8,128)(2,1)}, u32[]{:S(2)}, u32[]{:S(2)}) collective-permute-start(bf16[256,2048]{1,0:T(8,128)(2,1)} %slice.115), channel_id=1, source_target_pairs={{0,4},{1,5},{2,6},{3,7},{4,0},{5,1},{6,2},{7,3},{8,12},{9,13},{10,... | collective-permute-start | bytes 3145736 | tf_op jit(solution)/shard_map/ppermute | solution.py:492
  350.6 47.5 %collective-permute-start.26 = (bf16[256,2048]{1,0:T(8,128)(2,1)}, bf16[256,2048]{1,0:T(8,128)(2,1)}, u32[]{:S(2)}, u32[]{:S(2)}) collective-permute-start(bf16[256,2048]{1,0:T(8,128)(2,1)} %convolution_convert_fusion.4), channel_id=1, source_target_pairs={{0,4},{1,5},{2,6},{3,7},{4,0},{5,1},{6,2},{7,3},{8,12},{9,13},{10,... | collective-permute-start | bytes 3145736 | tf_op jit(solution)/shard_map/ppermute | solution.py:492
  402.2 27.3 %collective-permute-start.27 = (bf16[1024,576]{0,1:T(8,128)(2,1)}, bf16[1024,576]{0,1:T(8,128)(2,1)}, u32[]{:S(2)}, u32[]{:S(2)}) collective-permute-start(bf16[1024,576]{0,1:T(8,128)(2,1)} %fusion.29), channel_id=1, source_target_pairs={{0,4},{1,5},{2,6},{3,7},{4,0},{5,1},{6,2},{7,3},{8,12},{9,13},{10,... | collective-permute-start | bytes 3538952 | tf_op jit(solution)/shard_map/ppermute | solution.py:492
  402.5 37.8 %collective-permute-start.32 = (bf16[320,2048]{1,0:T(8,128)(2,1)}, bf16[320,2048]{1,0:T(8,128)(2,1)}, u32[]{:S(2)}, u32[]{:S(2)}) collective-permute-start(bf16[320,2048]{1,0:T(8,128)(2,1)} %add_convert_fusion.5), channel_id=1, source_target_pairs={{0,2},{1,3},{2,0},{3,1},{4,6},{5,7},{6,4},{7,5},{8,10},{9,11},{10,... | collective-permute-start | bytes 3932168 | tf_op jit(solution)/shard_map/ppermute | solution.py:492
  409.3 61.6 %collective-permute-start.31 = (bf16[2,256,2048]{2,1,0:T(8,128)(2,1)}, bf16[2,256,2048]{2,1,0:T(8,128)(2,1)}, u32[]{:S(2)}, u32[]{:S(2)}) collective-permute-start(bf16[2,256,2048]{2,1,0:T(8,128)(2,1)} %dynamic-slice_bitcast_fusion), channel_id=1, source_target_pairs={{0,1},{1,0},{2,3},{3,2},{4,5},{5,4},{6,7},{7,6},{8,9},{9,8},{10,11... | collective-permute-start | bytes 6291464 | tf_op jit(solution)/shard_map/ppermute | solution.py:492
  414.1 42.9 %collective-permute-start.30 = (bf16[256,2048]{1,0:T(8,128)(2,1)}, bf16[256,2048]{1,0:T(8,128)(2,1)}, u32[]{:S(2)}, u32[]{:S(2)}) collective-permute-start(bf16[256,2048]{1,0:T(8,128)(2,1)} %fusion.13), channel_id=1, source_target_pairs={{0,2},{1,3},{2,0},{3,1},{4,6},{5,7},{6,4},{7,5},{8,10},{9,11},{10,... | collective-permute-start | bytes 3145736 | tf_op jit(solution)/shard_map/ppermute | solution.py:492
  436.5 32.3 %all-to-all-start.4 = ((bf16[4,4,64,576]{3,2,1,0:T(8,128)(2,1)}), bf16[4,4,64,576]{3,2,1,0:T(8,128)(2,1)S(1)}, u32[]{:S(2)}, u32[]{:S(2)}) async-start(bf16[4,4,64,576]{3,2,1,0:T(8,128)(2,1)} %bitcast.192), calls=%async_computation.6 | async-start | bytes 2621440 | tf_op jit(solution)/shard_map/all_to_all | solution.py:742
  443.6 32.9 %collective-permute-start.34 = (bf16[4,40,2048]{2,1,0:T(8,128)(2,1)}, bf16[4,40,2048]{2,1,0:T(8,128)(2,1)}, u32[]{:S(2)}, u32[]{:S(2)}) collective-permute-start(bf16[4,40,2048]{2,1,0:T(8,128)(2,1)} %bitcast.51), channel_id=1, source_target_pairs={{0,4},{1,5},{2,6},{3,7},{4,0},{5,1},{6,2},{7,3},{8,12},{9,13},{10,... | collective-permute-start | bytes 1966088 | tf_op jit(solution)/shard_map/ppermute | solution.py:492
  475.3 27.8 %collective-permute-start.33 = (bf16[256,2048]{1,0:T(8,128)(2,1)}, bf16[256,2048]{1,0:T(8,128)(2,1)}, u32[]{:S(2)}, u32[]{:S(2)}) collective-permute-start(bf16[256,2048]{1,0:T(8,128)(2,1)} %dynamic-slice_bitcast_fusion.1), channel_id=1, source_target_pairs={{0,2},{1,3},{2,0},{3,1},{4,6},{5,7},{6,4},{7,5},{8,10},{9,11},{10,... | collective-permute-start | bytes 3145736 | tf_op jit(solution)/shard_map/ppermute | solution.py:492
  497.8 40.9 %all-to-all-start.5 = ((bf16[4,64,1920]{2,1,0:T(8,128)(2,1)}), bf16[4,64,1920]{2,1,0:T(8,128)(2,1)}, u32[]{:S(2)}, u32[]{:S(2)}) async-start(bf16[4,64,1920]{2,1,0:T(8,128)(2,1)} %join_columns.1), calls=%async_computation.8 | async-start | bytes 1966080 | tf_op jit(solution)/shard_map/all_to_all | solution.py:752
  (144 other events, 1543.3 us)
Sparse Core Ops, SparseCore 0:
  57.8 59.5 all-gather.5
  119.6 59.0 all-gather.7
  180.4 59.1 all-gather.3
  252.6 62.3 reduce-scatter.3
  317.1 63.2 reduce-scatter.5
  382.6 63.2 reduce-scatter.7
